TPU v7x, 128 devices: a whole 4x4x4 slice. The times are simulated.
128 devices in a mesh: stream: 32 (over x, y, core), radial: 4 (over z).
Axes of the slice: x: 4, y: 4, z: 4, core: 2. Of those that a mesh axis runs over, the one named last changes fastest.
Arguments:
- right_side: float32 [5, 4, 512, 64, 128], P(None, None, 'stream', 'radial'), may hold values from -18 to 18
- diag_block: float32 [5, 5, 512, 64, 128], P(None, None, 'stream', 'radial'), may hold values from -1.5 to 9.5
- face_coef: float32 [6, 512, 64, 128], P(None, 'stream', 'radial'), may hold values from 0.5 to 1.5
- jacobians: float32 [6, 5, 5], replicated, may hold values from -2.4 to 2.4
Outputs:
- basis_q: float32 [5, 16, 512, 64, 128], P(None, None, 'stream', 'radial')
- r_factor: float32 [16, 16], replicated
All inputs are finite; a program needn't handle non-finite values.
Results may differ from a plain program's by a relative error of at most 0.00023.
Values sent between devices are 32-bit elements; how exact they have to be, the bound alone decides.
A program may use at most 192 MiB of HBM per device.

v0:
```python
import jax
import jax.numpy as jnp
from jax import lax
from jax.sharding import PartitionSpec as P

NV = 5
POWERS = 3
NCOL = 16


shift_value = 6.0


def padded_2(cells, sides, width):
    for axis, dim in sides:
        count = lax.axis_size(axis)
        ends = count - 1
        head = lax.slice_in_dim(cells, 0, width, axis=dim)
        tail = lax.slice_in_dim(cells, cells.shape[dim] - width, cells.shape[dim], axis=dim)
        cells = jnp.concatenate(
            [
                lax.ppermute(tail, axis, [(i, (i + 1) % count) for i in range(ends)]),
                cells,
                lax.ppermute(head, axis, [((i + 1) % count, i) for i in range(ends)]),
            ],
            axis=dim,
        )
    return cells


def operate(padded, blocks, face_vals, jacobians):
    centre = padded[:, :, 1:-1, 1:-1]
    result = -shift_value * centre
    for column in range(centre.shape[0]):
        result = result + blocks[:, column][:, None] * centre[column][None]
    beside_list = (
        padded[:, :, :-2, 1:-1],
        padded[:, :, 2:, 1:-1],
        padded[:, :, 1:-1, :-2],
        padded[:, :, 1:-1, 2:],
        jnp.roll(centre, 1, axis=4),
        jnp.roll(centre, -1, axis=4),
    )
    for direction in range(6):
        coupled = jnp.einsum(
            "ab,brxyz->arxyz",
            jacobians[direction],
            beside_list[direction],
            precision=lax.Precision.HIGHEST,
        )
        result = result - face_vals[direction][None, None] * coupled
    return result


def unit_columns(vector):
    totals = lax.psum(jnp.sum(vector * vector, axis=(0, 2, 3, 4)), ("stream", "radial"))
    return vector / jnp.sqrt(totals)[None, :, None, None, None]


def upper_factor(gram_sums):
    order_size = gram_sums.shape[0]
    positions = jnp.arange(order_size)
    factor_rows = []
    for row_number in range(order_size):
        pending = gram_sums[row_number]
        for prior_row in range(row_number):
            pending = pending - factor_rows[prior_row][row_number] * factor_rows[prior_row]
        pivot_root = jnp.sqrt(pending[row_number])
        factor_rows.append(
            jnp.where(positions >= row_number, pending / pivot_root, jnp.zeros_like(pending))
        )
    return jnp.stack(factor_rows)


def upper_inverse(factor):
    order_size = factor.shape[0]
    identity = jnp.eye(order_size, dtype=factor.dtype)
    solved = [None] * order_size
    for row_number in reversed(range(order_size)):
        pending = identity[row_number]
        for later_row in range(row_number + 1, order_size):
            pending = pending - factor[row_number, later_row] * solved[later_row]
        solved[row_number] = pending / factor[row_number, row_number]
    return jnp.stack(solved)


def body(right_side, diag_block, face_coef, jacobians):
    current = unit_columns(right_side)
    columns = [current]
    for power_k in range(POWERS):
        padded = padded_2(current, (("stream", 2), ("radial", 3)), 1)
        current = unit_columns(operate(padded, diag_block, face_coef, jacobians))
        columns.append(current)
    stacked_cols = jnp.stack(columns, axis=1)
    basis_cols = stacked_cols.reshape(
        NV, NCOL, stacked_cols.shape[3], stacked_cols.shape[4], stacked_cols.shape[5]
    )
    local_gram = jnp.einsum(
        "acxyz,adxyz->cd", basis_cols, basis_cols, precision=lax.Precision.HIGHEST
    )
    gram_sums = lax.psum(local_gram, ("stream", "radial"))
    r_factor = upper_factor(gram_sums)
    inverse = upper_inverse(r_factor)
    basis_q = jnp.einsum("aixyz,ij->ajxyz", basis_cols, inverse, precision=lax.Precision.HIGHEST)
    return (basis_q, r_factor)


def solution(mesh):
    return jax.shard_map(
        body,
        mesh=mesh,
        in_specs=(
            P(None, None, "stream", "radial", None),
            P(None, None, "stream", "radial", None),
            P(None, "stream", "radial", None),
            P(),
        ),
        out_specs=(P(None, None, "stream", "radial", None), P()),
        check_vma=False,
    )
```

profile of v0, /device:TPU:1, one launch (start us, length us, event | category | flops | bytes accessed | tf_op | source)
XLA Modules:
  0.0 945.1 jit_solution(2283254332507579355)
XLA Ops:
  0.6 2.2 multiply_reduce_fusion.3
  2.9 68.6 %psum.35 = f32[4]{0:T(128)S(1)} all-reduce(f32[4]{0:T(128)S(1)} %multiply_reduce_fusion.3), channel_id=1, replica_groups=mesh['stream'=32,'radial'=4] {'stream','radial'}, use_global_device_ids=true, to_apply=%region_1.0 | all-reduce | flops 4 | bytes 32 | tf_op jit(solution)/shard_map/psum | solution.py:56
  71.5 3.7 fusion.215
  76.1 2.8 collective-permute-start.1
  78.9 3.0 collective-permute-start
  85.4 3.1 fusion.238
  88.9 6.1 fusion.80
  95.0 6.0 fusion.76
  107.6 4.5 collective-permute-start.2
  112.1 5.3 fusion.56
  117.4 5.3 fusion.52
  122.8 5.2 fusion.4
  128.7 17.8 %multiply_reduce_fusion.2 = (f32[4]{0:T(128)S(1)}, f32[5,4,16,16,128]{4,0,3,2,1:T(8,128)}) fusion(f32[4,16,16,128,5]{3,4,2,1,0:T(8,128)} %fusion.80, f32[16,16,128]{2,1,0:T(8,128)S(1)} %get-tuple-element.97, f32[4,16,16,128,5]{3,4,2,1,0:T(8,128)} %fusion.76, f32[16,16,128]{2,1,0:T(8,128)S(1)} %get-tuple-element.98, f32[1,5,5]{2,0,1:T(1,128)S(1)} %get-tuple-element.99, ...), kind=kOutput, calls=%fused_computation.123 | convolution fusion | flops 58055676 | bytes 25546868 | tf_op jit(solution)/shard_map/ab,brxyz->arxyz/dot_general | solution.py:45
  146.5 64.4 %psum.36 = f32[4]{0:T(128)S(1)} all-reduce(f32[4]{0:T(128)S(1)} %get-tuple-element.344), channel_id=1, replica_groups=mesh['stream'=32,'radial'=4] {'stream','radial'}, use_global_device_ids=true, to_apply=%region_3.4 | all-reduce | flops 4 | bytes 32 | tf_op jit(solution)/shard_map/psum | solution.py:56
  210.9 2.7 broadcast_divide_fusion.1
  217.1 3.1 fusion.234
  220.3 2.5 fusion.271
  222.8 2.8 collective-permute-start.5
  225.6 2.8 collective-permute-start.4
  228.4 6.1 fusion.88
  234.5 6.1 fusion.84
  241.9 4.2 collective-permute-start.6
  246.1 5.3 fusion.64
  251.4 5.3 fusion.60
  256.8 5.2 fusion.20
  262.8 17.6 %multiply_reduce_fusion.1 = (f32[4]{0:T(128)S(1)}, f32[5,4,16,16,128]{4,0,3,2,1:T(8,128)}) fusion(f32[4,16,16,128,5]{3,4,2,1,0:T(8,128)} %fusion.88, f32[16,16,128]{2,1,0:T(8,128)S(1)} %copy-done.25, f32[4,16,16,128,5]{3,4,2,1,0:T(8,128)} %fusion.84, f32[16,16,128]{2,1,0:T(8,128)S(1)} %copy-done.28, f32[1,5,5]{2,0,1:T(1,128)S(1)} %get-tuple-element.99, ...), kind=kOutput, calls=%fused_computation.122 | convolution fusion | flops 58055676 | bytes 25546868 | tf_op jit(solution)/shard_map/ab,brxyz->arxyz/dot_general | solution.py:45
  280.4 64.9 %psum.37 = f32[4]{0:T(128)S(1)} all-reduce(f32[4]{0:T(128)S(1)} %get-tuple-element.346), channel_id=1, replica_groups=mesh['stream'=32,'radial'=4] {'stream','radial'}, use_global_device_ids=true, to_apply=%region_5.6 | all-reduce | flops 4 | bytes 32 | tf_op jit(solution)/shard_map/psum | solution.py:56
  345.3 2.7 broadcast_divide_fusion
  349.8 1.7 fusion.233
  351.5 3.1 fusion.230
  354.7 2.5 fusion.272
  357.2 2.7 collective-permute-start.9
  359.9 2.9 collective-permute-start.8
  362.8 6.0 fusion.96
  368.8 6.1 fusion.92
  376.2 4.2 collective-permute-start.10
  380.4 5.3 fusion.72
  385.7 5.3 fusion.68
  391.1 5.2 fusion.36
  397.1 17.6 %multiply_reduce_fusion = (f32[4]{0:T(128)S(1)}, f32[5,4,16,16,128]{4,0,3,2,1:T(8,128)}) fusion(f32[4,16,16,128,5]{3,4,2,1,0:T(8,128)} %fusion.96, f32[16,16,128]{2,1,0:T(8,128)S(1)} %copy-done.26, f32[4,16,16,128,5]{3,4,2,1,0:T(8,128)} %fusion.92, f32[16,16,128]{2,1,0:T(8,128)S(1)} %copy-done.29, f32[1,5,5]{2,0,1:T(1,128)S(1)} %get-tuple-element.99, ...), kind=kOutput, calls=%fused_computation.121 | convolution fusion | flops 58055676 | bytes 25546868 | tf_op jit(solution)/shard_map/ab,brxyz->arxyz/dot_general | solution.py:45
  414.7 64.7 %psum.38 = f32[4]{0:T(128)S(1)} all-reduce(f32[4]{0:T(128)S(1)} %get-tuple-element.348), channel_id=1, replica_groups=mesh['stream'=32,'radial'=4] {'stream','radial'}, use_global_device_ids=true, to_apply=%region_7.8 | all-reduce | flops 4 | bytes 32 | tf_op jit(solution)/shard_map/psum | solution.py:56
  479.4 2.9 divide_bitcast_fusion
  484.1 8.1 pad_maximum_fusion
  492.2 32.5 %fusion.109 = f32[16,16]{1,0:T(8,128)S(1)} fusion(f32[5,16,16,16,128]{4,0,3,2,1:T(8,128)} %bitcast.933), kind=kOutput, calls=%fused_computation.128 | convolution fusion | flops 503316480 | bytes 10486784 | tf_op jit(solution)/shard_map/acxyz,adxyz->cd/dot_general | solution.py:98
  524.7 62.6 %psum.39 = f32[16,16]{1,0:T(8,128)S(1)} all-reduce(f32[16,16]{1,0:T(8,128)S(1)} %fusion.109), channel_id=1, replica_groups=mesh['stream'=32,'radial'=4] {'stream','radial'}, use_global_device_ids=true, to_apply=%region_8.9 | all-reduce | flops 256 | bytes 2048 | tf_op jit(solution)/shard_map/psum | solution.py:101
  595.1 1.8 fusion.187
  598.8 2.7 fusion.183
  603.4 3.0 fusion.178
  608.5 3.6 multiply_subtract_fusion.9
  614.2 4.4 multiply_subtract_fusion.8
  620.5 4.9 multiply_subtract_fusion.7
  627.2 5.8 multiply_subtract_fusion.6
  635.1 6.1 multiply_subtract_fusion.5
  643.2 6.7 multiply_subtract_fusion.4
  651.7 7.4 multiply_subtract_fusion.3
  661.0 8.2 multiply_subtract_fusion.2
  671.2 8.9 multiply_subtract_fusion.1
  682.1 9.5 %multiply_subtract_fusion = f32[16]{0:T(128)S(1)} fusion(f32[]{:T(128)} %bitcast.254, f32[]{:T(128)} %bitcast.253, f32[]{:T(128)} %bitcast.252, f32[]{:T(128)} %bitcast.251, f32[]{:T(128)} %bitcast.250, f32[]{:T(128)} %bitcast.249, f32[]{:T(128)} %bitcast.248, f32[]{:T(128)} %bitcast.247, f32[]{:T(128)} %bitcast.246, f32[]{:T(128)} %bitcast.245, ...), kind=kLoop, calls=%fused_computation.369 | loop fusion | flops 1152 | bytes 1204 | tf_op jit(solution)/shard_map/sub | solution.py:67
  692.9 74.5 %compare_select_fusion.1 = (f32[1,16]{1,0:T(1,128)S(1)}, f32[1,16]{1,0:T(1,128)S(1)}, f32[1,16]{1,0:T(1,128)S(1)}, f32[1,16]{1,0:T(1,128)S(1)}, f32[1,16]{1,0:T(...) fusion(f32[]{:T(128)} %bitcast.256, ...), kind=kLoop, calls=%fused_computation.159 | loop fusion | flops 4528 | bytes 2456 | tf_op jit(solution)/shard_map/jit(_where)/select_n | solution.py:70
  776.3 65.6 %subtract_divide_fusion = (f32[1,16]{1,0:T(1,128)S(1)}, f32[1,16]{1,0:T(1,128)S(1)}, f32[1,16]{1,0:T(1,128)S(1)}, f32[1,16]{1,0:T(1,128)S(1)}, f32[1,16]{1,0:T(1...) fusion(f32[16,16]{1,0:T(8,128)S(1)} %fusion.113, ...), kind=kLoop, calls=%fused_computation.359 | loop fusion | flops 3136 | bytes 2276 | tf_op jit(solution)/shard_map/div | solution.py:83
  841.9 58.1 %fusion.127 = (f32[16]{0:T(128)S(1)}, f32[16]{0:T(128)S(1)}, f32[16]{0:T(128)S(1)}, f32[16]{0:T(128)S(1)}, f32[16]{0:T(128)S(1)}, /*index=5*/f32[16]{0:T(128)S(1...) fusion(f32[16,16]{1,0:T(8,128)S(1)} %fusion.113, f32[1,16]{1,0:T(1,128)S(1)} %get-tuple-element.15, ...), kind=kLoop, calls=%fused_computation.232 | loop fusion | flops 2816 | bytes 1908 | tf_op jit(solution)/shard_map/div | solution.py:83
  900.0 19.3 %fusion.196 = (f32[1,16]{1,0:T(1,128)S(1)}, f32[16]{0:T(128)S(1)}) fusion(f32[1,16]{1,0:T(1,128)S(1)} %get-tuple-element.18, f32[1,16]{1,0:T(1,128)S(1)} %get-tuple-element.17, f32[1,16]{1,0:T(1,128)S(1)} %get-tuple-element.16, f32[1,16]{1,0:T(1,128)S(1)} %get-tuple-element.15, f32[16]{0:T(128)S(1)} %get-tuple-element.32, f32[16]{0:T(128)S(1)} %get-tuple-element.31, ...), kind=kLoop, calls=%fused_computation.381 | loop fusion | flops 960 | bytes 1276 | tf_op jit(solution)/shard_map/stack | solution.py:84
  919.4 18.3 %fusion.100 = f32[5,16,16,16,128]{4,1,3,2,0:T(8,128)S(1)} fusion(f32[5,16,16,16,128]{4,0,3,2,1:T(8,128)} %bitcast.934, f32[16,16]{1,0:T(8,128)S(1)} %stack.25), kind=kOutput, calls=%fused_computation.124 | convolution fusion | flops 503316480 | bytes 20972544 | tf_op jit(solution)/shard_map/aixyz,ij->ajxyz/dot_general | solution.py:104
  937.6 7.3 copy.22
  (171 shorter events, 53.9 us)
Async XLA Ops:
  0.6 70.9 %copy-start.10 = (f32[5,4,16,16,128]{4,3,2,1,0:T(8,128)S(1)}, f32[5,4,16,16,128]{4,3,2,1,0:T(8,128)}, u32[]{:S(2)}) copy-start(f32[5,4,16,16,128]{4,3,2,1,0:T(8,128)} %param.4) | copy-start | bytes 7864324
  75.2 47.6 %copy-start = (f32[5,4,16,16,128]{4,0,3,2,1:T(8,128)}, f32[5,4,16,16,128]{4,0,3,2,1:T(8,128)S(1)}, u32[]{:S(2)}) copy-start(f32[5,4,16,16,128]{4,0,3,2,1:T(8,128)S(1)} %get-tuple-element.92) | copy-start | bytes 7864324
  76.1 30.2 %collective-permute-start.1 = (f32[5,4,1,16,128]{4,0,3,2,1:T(8,128)}, f32[5,4,1,16,128]{4,0,3,2,1:T(8,128)S(1)}, u32[]{:S(2)}, u32[]{:S(2)}) collective-permute-start(f32[5,4,1,16,128]{4,0,3,2,1:T(8,128)} %get-tuple-element.81), channel_id=1, source_target_pairs={{4,0},{8,4},{12,8},{16,12},{20,16},{24,20},{28,24},{32,28},{36,32}... | collective-permute-start | bytes 491528 | tf_op jit(solution)/shard_map/ppermute | solution.py:24
  78.9 27.4 %collective-permute-start = (f32[5,4,1,16,128]{4,0,3,2,1:T(8,128)}, f32[5,4,1,16,128]{4,0,3,2,1:T(8,128)S(1)}, u32[]{:S(2)}, u32[]{:S(2)}) collective-permute-start(f32[5,4,1,16,128]{4,0,3,2,1:T(8,128)} %get-tuple-element.80), channel_id=1, source_target_pairs={{0,4},{4,8},{8,12},{12,16},{16,20},{20,24},{24,28},{28,32},{32,36}... | collective-permute-start | bytes 491528 | tf_op jit(solution)/shard_map/ppermute | solution.py:22
  85.4 3.2 copy-start.34
  85.4 3.2 copy-start.11
  95.0 6.0 copy-start.30
  101.1 27.6 %copy-start.12 = (f32[16,16,128]{2,1,0:T(8,128)}, f32[16,16,128]{2,1,0:T(8,128)S(1)}, u32[]{:S(2)}) copy-start(f32[16,16,128]{2,1,0:T(8,128)S(1)} %get-tuple-element.93) | copy-start | bytes 393220
  101.1 27.6 %copy-start.15 = (f32[16,16,128]{2,1,0:T(8,128)}, f32[16,16,128]{2,1,0:T(8,128)S(1)}, u32[]{:S(2)}) copy-start(f32[16,16,128]{2,1,0:T(8,128)S(1)} %get-tuple-element.94) | copy-start | bytes 393220
  101.1 27.6 %copy-start.18 = (f32[16,16,128]{2,1,0:T(8,128)}, f32[16,16,128]{2,1,0:T(8,128)S(1)}, u32[]{:S(2)}) copy-start(f32[16,16,128]{2,1,0:T(8,128)S(1)} %get-tuple-element.95) | copy-start | bytes 393220
  101.1 27.6 %copy-start.21 = (f32[16,16,128]{2,1,0:T(8,128)}, f32[16,16,128]{2,1,0:T(8,128)S(1)}, u32[]{:S(2)}) copy-start(f32[16,16,128]{2,1,0:T(8,128)S(1)} %get-tuple-element.96) | copy-start | bytes 393220
  101.1 27.6 %copy-start.24 = (f32[16,16,128]{2,1,0:T(8,128)}, f32[16,16,128]{2,1,0:T(8,128)S(1)}, u32[]{:S(2)}) copy-start(f32[16,16,128]{2,1,0:T(8,128)S(1)} %get-tuple-element.97) | copy-start | bytes 393220
  101.1 27.6 %copy-start.27 = (f32[16,16,128]{2,1,0:T(8,128)}, f32[16,16,128]{2,1,0:T(8,128)S(1)}, u32[]{:S(2)}) copy-start(f32[16,16,128]{2,1,0:T(8,128)S(1)} %get-tuple-element.98) | copy-start | bytes 393220
  102.0 26.7 %copy-start.7 = (f32[5,16,16,128]{3,0,2,1:T(8,128)}, f32[5,16,16,128]{3,0,2,1:T(8,128)S(1)}, u32[]{:S(2)}) copy-start(f32[5,16,16,128]{3,0,2,1:T(8,128)S(1)} %copy.10) | copy-start | bytes 1966084
  106.3 21.7 %collective-permute-start.3 = (f32[5,4,18,1,128]{4,0,3,2,1:T(8,128)S(1)}, f32[5,4,18,1,128]{4,0,3,2,1:T(8,128)S(1)}, u32[]{:S(2)}, u32[]{:S(2)}) collective-permute-start(f32[5,4,18,1,128]{4,0,3,2,1:T(8,128)S(1)} %get-tuple-element.51), channel_id=1, source_target_pairs={{1,0},{2,1},{3,2},{5,4},{6,5},{7,6},{9,8},{10,9},{11,10},{13,12},{... | collective-permute-start | bytes 552968 | tf_op jit(solution)/shard_map/ppermute | solution.py:24
  107.6 15.1 %collective-permute-start.2 = (f32[5,4,18,1,128]{4,0,3,2,1:T(8,128)S(1)}, f32[5,4,18,1,128]{4,0,3,2,1:T(8,128)S(1)}, u32[]{:S(2)}, u32[]{:S(2)}) collective-permute-start(f32[5,4,18,1,128]{4,0,3,2,1:T(8,128)S(1)} %get-tuple-element.52), channel_id=1, source_target_pairs={{0,1},{1,2},{2,3},{4,5},{5,6},{6,7},{8,9},{9,10},{10,11},{12,13},{... | collective-permute-start | bytes 552968 | tf_op jit(solution)/shard_map/ppermute | solution.py:22
  128.0 0.7 copy-start.32
  213.6 43.2 %copy-start.2 = (f32[5,4,16,16,128]{4,0,3,2,1:T(8,128)}, f32[5,4,16,16,128]{4,0,3,2,1:T(8,128)S(1)}, u32[]{:S(2)}) copy-start(f32[5,4,16,16,128]{4,0,3,2,1:T(8,128)S(1)} %broadcast_divide_fusion.1) | copy-start | bytes 7864324
  217.1 3.2 copy-start.3
  222.8 17.7 %collective-permute-start.5 = (f32[5,4,1,16,128]{4,0,3,2,1:T(8,128)S(1)}, f32[5,4,1,16,128]{4,0,3,2,1:T(8,128)S(1)}, u32[]{:S(2)}, u32[]{:S(2)}) collective-permute-start(f32[5,4,1,16,128]{4,0,3,2,1:T(8,128)S(1)} %get-tuple-element.70), channel_id=1, source_target_pairs={{4,0},{8,4},{12,8},{16,12},{20,16},{24,20},{28,24},{32,28},{36,32}... | collective-permute-start | bytes 491528 | tf_op jit(solution)/shard_map/ppermute | solution.py:24
  225.6 14.9 %collective-permute-start.4 = (f32[5,4,1,16,128]{4,0,3,2,1:T(8,128)S(1)}, f32[5,4,1,16,128]{4,0,3,2,1:T(8,128)S(1)}, u32[]{:S(2)}, u32[]{:S(2)}) collective-permute-start(f32[5,4,1,16,128]{4,0,3,2,1:T(8,128)S(1)} %get-tuple-element.69), channel_id=1, source_target_pairs={{0,4},{4,8},{8,12},{12,16},{16,20},{20,24},{24,28},{28,32},{32,36}... | collective-permute-start | bytes 491528 | tf_op jit(solution)/shard_map/ppermute | solution.py:22
  240.6 21.4 %collective-permute-start.7 = (f32[5,4,18,1,128]{4,0,3,2,1:T(8,128)S(1)}, f32[5,4,18,1,128]{4,0,3,2,1:T(8,128)S(1)}, u32[]{:S(2)}, u32[]{:S(2)}) collective-permute-start(f32[5,4,18,1,128]{4,0,3,2,1:T(8,128)S(1)} %get-tuple-element.49), channel_id=1, source_target_pairs={{1,0},{2,1},{3,2},{5,4},{6,5},{7,6},{9,8},{10,9},{11,10},{13,12},{... | collective-permute-start | bytes 552968 | tf_op jit(solution)/shard_map/ppermute | solution.py:24
  241.9 14.9 %collective-permute-start.6 = (f32[5,4,18,1,128]{4,0,3,2,1:T(8,128)S(1)}, f32[5,4,18,1,128]{4,0,3,2,1:T(8,128)S(1)}, u32[]{:S(2)}, u32[]{:S(2)}) collective-permute-start(f32[5,4,18,1,128]{4,0,3,2,1:T(8,128)S(1)} %get-tuple-element.50), channel_id=1, source_target_pairs={{0,1},{1,2},{2,3},{4,5},{5,6},{6,7},{8,9},{9,10},{10,11},{12,13},{... | collective-permute-start | bytes 552968 | tf_op jit(solution)/shard_map/ppermute | solution.py:22
  256.7 6.0 copy-start.8
  256.7 6.0 copy-start.13
  256.7 6.0 copy-start.16
  256.7 6.0 copy-start.19
  256.7 6.0 copy-start.22
  256.7 6.0 copy-start.25
  256.8 6.0 copy-start.28
  262.0 0.7 copy-start.33
  348.0 43.1 %copy-start.1 = (f32[5,4,16,16,128]{4,0,3,2,1:T(8,128)}, f32[5,4,16,16,128]{4,0,3,2,1:T(8,128)S(1)}, u32[]{:S(2)}) copy-start(f32[5,4,16,16,128]{4,0,3,2,1:T(8,128)S(1)} %broadcast_divide_fusion) | copy-start | bytes 7864324
  351.5 3.2 copy-start.4
  357.2 17.6 %collective-permute-start.9 = (f32[5,4,1,16,128]{4,0,3,2,1:T(8,128)S(1)}, f32[5,4,1,16,128]{4,0,3,2,1:T(8,128)S(1)}, u32[]{:S(2)}, u32[]{:S(2)}) collective-permute-start(f32[5,4,1,16,128]{4,0,3,2,1:T(8,128)S(1)} %get-tuple-element.59), channel_id=1, source_target_pairs={{4,0},{8,4},{12,8},{16,12},{20,16},{24,20},{28,24},{32,28},{36,32}... | collective-permute-start | bytes 491528 | tf_op jit(solution)/shard_map/ppermute | solution.py:24
  359.9 14.9 %collective-permute-start.8 = (f32[5,4,1,16,128]{4,0,3,2,1:T(8,128)S(1)}, f32[5,4,1,16,128]{4,0,3,2,1:T(8,128)S(1)}, u32[]{:S(2)}, u32[]{:S(2)}) collective-permute-start(f32[5,4,1,16,128]{4,0,3,2,1:T(8,128)S(1)} %get-tuple-element.58), channel_id=1, source_target_pairs={{0,4},{4,8},{8,12},{12,16},{16,20},{20,24},{24,28},{28,32},{32,36}... | collective-permute-start | bytes 491528 | tf_op jit(solution)/shard_map/ppermute | solution.py:22
  374.9 21.5 %collective-permute-start.11 = (f32[5,4,18,1,128]{4,0,3,2,1:T(8,128)S(1)}, f32[5,4,18,1,128]{4,0,3,2,1:T(8,128)S(1)}, u32[]{:S(2)}, u32[]{:S(2)}) collective-permute-start(f32[5,4,18,1,128]{4,0,3,2,1:T(8,128)S(1)} %get-tuple-element.47), channel_id=1, source_target_pairs={{1,0},{2,1},{3,2},{5,4},{6,5},{7,6},{9,8},{10,9},{11,10},{13,12},{... | collective-permute-start | bytes 552968 | tf_op jit(solution)/shard_map/ppermute | solution.py:24
  376.2 14.9 %collective-permute-start.10 = (f32[5,4,18,1,128]{4,0,3,2,1:T(8,128)S(1)}, f32[5,4,18,1,128]{4,0,3,2,1:T(8,128)S(1)}, u32[]{:S(2)}, u32[]{:S(2)}) collective-permute-start(f32[5,4,18,1,128]{4,0,3,2,1:T(8,128)S(1)} %get-tuple-element.48), channel_id=1, source_target_pairs={{0,1},{1,2},{2,3},{4,5},{5,6},{6,7},{8,9},{9,10},{10,11},{12,13},{... | collective-permute-start | bytes 552968 | tf_op jit(solution)/shard_map/ppermute | solution.py:22
  391.0 6.0 copy-start.9
  391.0 6.0 copy-start.14
  391.1 6.0 copy-start.17
  391.1 6.0 copy-start.20
  391.1 6.0 copy-start.23
  391.1 6.0 copy-start.26
  391.1 6.0 copy-start.29
  396.3 0.7 copy-start.31
  479.4 3.5 copy-start.5
  479.4 4.7 copy-start.6
where the time goes:
time: 953 us; the launch traced here: 945 us
  blocking collectives  325 us (34%)
  other arithmetic  320 us (34%)
  matrix products  188 us (20%)
  local copies, waits for them, and re-layouts  66.2 us (7%)
  starting transfers between devices  33.7 us (4%)
  between operations  12.1 us (1%)
    psum x4, blocking collectives, unit_columns(): lax.psum(jnp.sum(vector * vector, axis=(0, 2, 3, 4)), ('stream', 'radial'))  263 us
    dot_general x18, matrix products, operate(): jnp.einsum('ab,brxyz->arxyz', jacobians[direction], beside_list[direction...  137 us
    div x2, other arithmetic, upper_inverse(): solved[row_number] = pending / factor[row_number, row_number]  124 us
    sub x15, other arithmetic, upper_factor(): pending - factor_rows[prior_row][row_number] * factor_rows[prior_row]  75.1 us
    select_n x16, other arithmetic, upper_factor(): jnp.where(positions >= row_number, pending / pivot_root, jnp.zeros_like(p...  74.6 us
    psum x1, blocking collectives, body(): gram_sums = lax.psum(local_gram, ('stream', 'radial'))  62.6 us
    dot_general x1, matrix products, body(): jnp.einsum('acxyz,adxyz->cd', basis_cols, basis_cols, precision=lax.Preci...  32.5 us
    ppermute x6, starting transfers between devices, padded_2(): lax.ppermute(tail, axis, [(i, (i + 1) % count) for i in range(ends)])  21.6 us
  transfers between devices with their start and end apart: 12, of which 0 were waited for; matrix products, arithmetic and copies ran while one was open for 10% of the time, Pallas kernels for 0%

commit v1 on v0

v1 whole, which is shorter than its diff:
```python
import functools

import jax
import jax.numpy as jnp
from jax import lax
from jax.experimental import pallas as pl
from jax.experimental.pallas import tpu as pltpu
from jax.sharding import PartitionSpec as P

NV = 5
NRHS = 4
POWERS = 3
NCOL = 16
LS = 16
LR = 16
NT = 128
ROWS = LS * LR
SHIFT = 6.0
BLK = NV * LR
KDIM = 256
DIRS = ((0, 0), (1, 0), (2, -1), (3, 1), (4, 0), (5, 0), (2, 0), (3, 0))
RAISE = 2.0**24
MESH = pl.DeviceIdType.MESH
HIGH = lax.Precision.HIGHEST


def build_operator(jac_ref, w_ref):
    col = lax.broadcasted_iota(jnp.int32, (LR, KDIM), 1)
    row = lax.broadcasted_iota(jnp.int32, (LR, KDIM), 0)
    part = col // BLK
    var = (col % BLK) // LR
    cell = col % LR
    masks = {}
    for offset in (-1, 0, 1):
        hit = (cell == row + offset) & (part < 3)
        masks[offset] = [
            jnp.where(hit & (var == b), 1.0, 0.0).astype(jnp.float32) for b in range(NV)
        ]
    for block, (direction, offset) in enumerate(DIRS):
        for a in range(NV):
            total = jac_ref[direction, a, 0] * masks[offset][0]
            for b in range(1, NV):
                total = total + jac_ref[direction, a, b] * masks[offset][b]
            head = total.astype(jnp.bfloat16).astype(jnp.float32)
            mixed = jnp.where(part == 1, total - head, head)
            start = block * BLK + a * LR
            w_ref[start : start + LR, :] = mixed.astype(jnp.bfloat16)


def split_fields(values, x_ref):
    head = values.astype(jnp.bfloat16)
    tail = (values - head.astype(jnp.float32)).astype(jnp.bfloat16)
    for r in range(NRHS):
        lanes = slice(r * NT, (r + 1) * NT)
        head_r = head[:, r].reshape(BLK, NT)
        x_ref[0:BLK, lanes] = head_r
        x_ref[BLK : 2 * BLK, lanes] = head_r
        x_ref[2 * BLK : 3 * BLK, lanes] = tail[:, r].reshape(BLK, NT)


def piece(product, block, r):
    return product[block * BLK : (block + 1) * BLK, r * NT : (r + 1) * NT].reshape(NV, LR, NT)


def apply_inner(source, target, diag_ref, face_ref, w_ref, x_ref, q_ref, scale):
    target[:, :, 0:LR, :] = jnp.zeros((NV, NRHS, LR, NT), jnp.float32)
    target[:, :, ROWS : ROWS + LR, :] = jnp.zeros((NV, NRHS, LR, NT), jnp.float32)

    def step(s, carry):
        here = pl.ds(pl.multiple_of(s * LR, LR), LR)
        after = pl.ds(pl.multiple_of((s + 1) * LR, LR), LR)
        before = pl.ds(pl.multiple_of(((s + LS) % (LS + 1)) * LR, LR), LR)
        face_after = pl.ds(pl.multiple_of(jnp.minimum(s + 1, LS - 1) * LR, LR), LR)
        face_before = pl.ds(pl.multiple_of(jnp.maximum(s - 1, 0) * LR, LR), LR)
        values = source[:, :, here, :]
        split_fields(values, x_ref)
        q_ref[...] = jnp.dot(w_ref[0 : 6 * BLK, :], x_ref[...], preferred_element_type=jnp.float32)
        f0 = face_ref[0, face_after, :] * scale
        f1 = face_ref[1, face_before, :] * scale
        f2, f3, f4, f5 = (face_ref[d, here, :] for d in range(2, 6))
        for r in range(NRHS):
            mine = values[:, r]
            total = -SHIFT * mine
            for b in range(NV):
                total = total + diag_ref[:, b, here, :] * mine[b]
            total = total - f2 * piece(q_ref, 2, r)
            total = total - f3 * piece(q_ref, 3, r)
            total = total - f4 * pltpu.roll(piece(q_ref, 4, r), 1, 2)
            total = total - f5 * pltpu.roll(piece(q_ref, 5, r), NT - 1, 2)
            if scale != 1.0:
                total = total * scale
            target[:, r, here, :] = target[:, r, here, :] + total
            target[:, r, after, :] = -(f0 * piece(q_ref, 0, r))
            target[:, r, before, :] = target[:, r, before, :] - f1 * piece(q_ref, 1, r)
        return carry

    lax.fori_loop(0, LS, step, 0)


def add_halo(target, face_ref, w_ref, x_ref, slabs, edges, rows_ref, scale):
    for side in range(2):
        start = 0 if side == 0 else ROWS - LR
        split_fields(slabs[side], x_ref)
        product = jnp.dot(
            w_ref[side * BLK : (side + 1) * BLK, :], x_ref[...], preferred_element_type=jnp.float32
        )
        weight = face_ref[side, start : start + LR, :] * scale
        for r in range(NRHS):
            target[:, r, start : start + LR, :] = target[
                :, r, start : start + LR, :
            ] - weight * piece(product, 0, r)
    for side in range(2):
        rows = pl.ds(0 if side == 0 else LR - 1, LS, stride=LR)
        split_fields(edges[side], x_ref)
        product = jnp.dot(
            w_ref[(6 + side) * BLK : (7 + side) * BLK, :],
            x_ref[...],
            preferred_element_type=jnp.float32,
        )
        weight = face_ref[2 + side, rows, :] * scale
        for a in range(NV):
            for r in range(NRHS):
                fresh = target[a, r, rows, :] - weight * (
                    product[a * LR : (a + 1) * LR, r * NT : (r + 1) * NT]
                )
                target[a, r, rows, :] = fresh
                if rows_ref is not None:
                    rows_ref[side, a, r] = fresh


def local_gram(y_ref, m_ref):
    m_ref[...] = jnp.zeros((ROWS, ROWS), jnp.float32)

    def step(s, carry):
        here = pl.ds(pl.multiple_of(s * LR, LR), LR)
        left = []
        right = []
        for a in range(NV):
            values = jnp.concatenate(
                [y_ref[k, a, :, here, :].reshape(NRHS * LR, NT) for k in range(POWERS + 1)], axis=0
            )
            head = values.astype(jnp.bfloat16)
            tail = (2.0 * (values - head.astype(jnp.float32))).astype(jnp.bfloat16)
            left += [head, tail]
            right += [head, head]
        m_ref[...] += lax.dot_general(
            jnp.concatenate(left, axis=1),
            jnp.concatenate(right, axis=1),
            (((1,), (1,)), ((), ())),
            preferred_element_type=jnp.float32,
        )
        return carry

    lax.fori_loop(0, LS, step, 0)
    row = lax.broadcasted_iota(jnp.int32, (ROWS, ROWS), 0)
    col = lax.broadcasted_iota(jnp.int32, (ROWS, ROWS), 1)
    kept = jnp.where(row % LR == col % LR, m_ref[...], 0.0)
    pick_row = lax.broadcasted_iota(jnp.int32, (NCOL, ROWS), 0)
    pick_col = lax.broadcasted_iota(jnp.int32, (NCOL, ROWS), 1)
    pick = jnp.where(pick_col // LR == pick_row, 1.0, 0.0).astype(jnp.float32)
    wide_row = lax.broadcasted_iota(jnp.int32, (NT, ROWS), 0)
    wide_col = lax.broadcasted_iota(jnp.int32, (NT, ROWS), 1)
    wide = jnp.where(wide_col // LR == wide_row, 1.0, 0.0).astype(jnp.float32)
    half = jnp.dot(pick, kept, precision=HIGH, preferred_element_type=jnp.float32)
    return lax.dot_general(
        half, wide, (((1,), (1,)), ((), ())), precision=HIGH, preferred_element_type=jnp.float32
    )


def krylov_kernel(
    n_stream,
    n_radial,
    right_hbm,
    diag_hbm,
    face_hbm,
    jac_ref,
    y_hbm,
    gram_ref,
    y_ref,
    diag_ref,
    face_ref,
    w_ref,
    x_ref,
    q_ref,
    slab_ref,
    edge_ref,
    pack_ref,
    m_ref,
    first_ref,
    second_ref,
    load_sem,
    out_sem,
    halo_send,
    halo_recv,
    first_send,
    first_recv,
    second_send,
    second_recv,
):
    si = lax.axis_index("stream")
    ri = lax.axis_index("radial")
    core = si % 2
    chip = si // 2
    n_first = 2 * n_radial
    n_second = n_stream // 2
    me_first = ri * 2 + core

    def first_peer(offset):
        other = (me_first + offset) % n_first
        return (chip * 2 + other % 2, other // 2)

    def second_peer(offset):
        return (((chip + offset) % n_second) * 2 + core, ri)

    loads = [
        pltpu.make_async_copy(right_hbm, y_ref.at[0, :, :, pl.ds(0, ROWS), :], load_sem.at[0]),
        pltpu.make_async_copy(face_hbm, face_ref, load_sem.at[1]),
        pltpu.make_async_copy(diag_hbm, diag_ref, load_sem.at[2]),
    ]
    for load in loads:
        load.start()

    barrier = pltpu.get_barrier_semaphore()
    for offset in range(1, n_first):
        pl.semaphore_signal(barrier, inc=1, device_id=first_peer(offset), device_id_type=MESH)
    for offset in range(1, n_second):
        pl.semaphore_signal(barrier, inc=1, device_id=second_peer(offset), device_id_type=MESH)
    peers = ((si + 1, ri), (si - 1, ri), (si, ri + 1), (si, ri - 1))
    present = (si < n_stream - 1, si > 0, ri < n_radial - 1, ri > 0)
    source_of = (1, 0, 3, 2)
    for j in range(4):

        @pl.when(present[j])
        def _(j=j):
            pl.semaphore_signal(barrier, inc=1, device_id=peers[j], device_id_type=MESH)

    x_ref[3 * BLK :, :] = jnp.zeros((KDIM - 3 * BLK, NRHS * NT), jnp.bfloat16)
    build_operator(jac_ref, w_ref)
    for side in range(2):

        @pl.when(jnp.logical_not(present[1 - side]))
        def _(side=side):
            slab_ref[:, side] = jnp.zeros((POWERS, NV, NRHS, LR, NT), jnp.float32)

        @pl.when(jnp.logical_not(present[3 - side]))
        def _(side=side):
            edge_ref[:, side] = jnp.zeros((POWERS, NV, NRHS, LS, NT), jnp.float32)

    greeted = n_first - 1 + n_second - 1
    for j in range(4):
        greeted = greeted + present[j].astype(jnp.int32)
    pl.semaphore_wait(barrier, greeted)

    def halo_copy(k, j):
        if j < 2:
            start = ROWS - LR if j == 0 else 0
            whole = right_hbm if k == 0 else y_ref.at[k]
            src = whole.at[:, :, pl.ds(start, LR), :]
            dst = slab_ref.at[k, j]
        else:
            src = pack_ref.at[k, 3 - j]
            dst = edge_ref.at[k, j - 2]
        return pltpu.make_async_remote_copy(
            src_ref=src,
            dst_ref=dst,
            send_sem=halo_send.at[k, j],
            recv_sem=halo_recv.at[k, j],
            device_id=peers[j],
            device_id_type=MESH,
        )

    def send_halo(k, js):
        for j in js:

            @pl.when(present[j])
            def _(j=j):
                halo_copy(k, j).start()

    def wait_halo(k):
        for j in range(4):

            @pl.when(present[source_of[j]])
            def _(j=j):
                halo_copy(k, j).wait_recv()

    send_halo(0, (0, 1))
    loads[0].wait()
    for side in range(2):
        rows = pl.ds(0 if side == 0 else LR - 1, LS, stride=LR)
        for a in range(NV):
            for r in range(NRHS):
                pack_ref[0, side, a, r] = y_ref[0, a, r, rows, :]
    send_halo(0, (2, 3))
    loads[1].wait()
    loads[2].wait()

    stores = []
    for k in range(POWERS):
        scale = RAISE if k == 0 else 1.0
        target = y_ref.at[k + 1]
        apply_inner(y_ref.at[k], target, diag_ref, face_ref, w_ref, x_ref, q_ref, scale)
        wait_halo(k)
        last = k == POWERS - 1
        add_halo(
            target,
            face_ref,
            w_ref,
            x_ref,
            (slab_ref[k, 0], slab_ref[k, 1]),
            (edge_ref[k, 0], edge_ref[k, 1]),
            None if last else pack_ref.at[k + 1],
            scale,
        )
        if not last:
            send_halo(k + 1, range(4))
        store = pltpu.make_async_copy(
            target.at[:, :, pl.ds(0, ROWS), :], y_hbm.at[k], out_sem.at[k]
        )
        store.start()
        stores.append(store)

    def reduce_over(value, slots, send, recv, count, me, peer):
        slots[me] = value
        copies = []
        for offset in range(1, count):
            copies.append(
                pltpu.make_async_remote_copy(
                    src_ref=slots.at[me],
                    dst_ref=slots.at[me],
                    send_sem=send.at[offset],
                    recv_sem=recv.at[offset],
                    device_id=peer(offset),
                    device_id_type=MESH,
                )
            )
        for copy in copies:
            copy.start()
        for copy in copies:
            copy.wait()
        total = slots[0]
        for index in range(1, count):
            total = total + slots[index]
        return total

    gram = local_gram(y_ref, m_ref)
    gram = reduce_over(gram, first_ref, first_send, first_recv, n_first, me_first, first_peer)
    gram = reduce_over(gram, second_ref, second_send, second_recv, n_second, chip, second_peer)
    gram_ref[...] = gram
    for k in range(POWERS):
        for j in range(4):

            @pl.when(present[j])
            def _(k=k, j=j):
                halo_copy(k, j).wait_send()

    for store in stores:
        store.wait()


def krylov(n_stream, n_radial, right, diag, face, jac):
    any_spec = pl.BlockSpec(memory_space=pl.ANY)
    f32 = jnp.float32
    dma = pltpu.SemaphoreType.DMA
    n_first = 2 * n_radial
    n_second = n_stream // 2
    return pl.pallas_call(
        functools.partial(krylov_kernel, n_stream, n_radial),
        out_shape=(
            jax.ShapeDtypeStruct((POWERS, NV, NRHS, ROWS, NT), f32),
            jax.ShapeDtypeStruct((NCOL, NT), f32),
        ),
        in_specs=[any_spec, any_spec, any_spec, pl.BlockSpec(memory_space=pltpu.SMEM)],
        out_specs=(any_spec, pl.BlockSpec(memory_space=pltpu.VMEM)),
        scratch_shapes=[
            pltpu.VMEM((POWERS + 1, NV, NRHS, ROWS + LR, NT), f32),
            pltpu.VMEM((NV, NV, ROWS, NT), f32),
            pltpu.VMEM((6, ROWS, NT), f32),
            pltpu.VMEM((len(DIRS) * BLK, KDIM), jnp.bfloat16),
            pltpu.VMEM((KDIM, NRHS * NT), jnp.bfloat16),
            pltpu.VMEM((6 * BLK, NRHS * NT), f32),
            pltpu.VMEM((POWERS, 2, NV, NRHS, LR, NT), f32),
            pltpu.VMEM((POWERS, 2, NV, NRHS, LS, NT), f32),
            pltpu.VMEM((POWERS, 2, NV, NRHS, LS, NT), f32),
            pltpu.VMEM((ROWS, ROWS), f32),
            pltpu.VMEM((n_first, NCOL, NT), f32),
            pltpu.VMEM((n_second, NCOL, NT), f32),
            dma((3,)),
            dma((POWERS,)),
            dma((POWERS, 4)),
            dma((POWERS, 4)),
            dma((n_first,)),
            dma((n_first,)),
            dma((n_second,)),
            dma((n_second,)),
        ],
        compiler_params=pltpu.CompilerParams(collective_id=0, has_side_effects=True),
    )(right, diag, face, jac)


def factor(gram_ref, r_ref, c_ref):
    row = lax.broadcasted_iota(jnp.int32, (NCOL, NT), 0)
    col = lax.broadcasted_iota(jnp.int32, (NCOL, NT), 1)
    twice = gram_ref[...]
    gram = 0.5 * (twice[:, :NCOL] + twice[:, :NCOL].T)
    gram = jnp.concatenate([gram, jnp.zeros((NCOL, NT - NCOL), jnp.float32)], axis=1)
    on_diag = jnp.where(row == col, gram, 0.0)
    down = 1.0 / jnp.sqrt(jnp.sum(on_diag, axis=1, keepdims=True))
    across = jnp.sum(on_diag, axis=0, keepdims=True)
    across = 1.0 / jnp.sqrt(jnp.where(col[:1] < NCOL, across, 1.0))
    work = gram * down * across
    work = jnp.where(col == row + NCOL, 1.0, work)
    for i in range(NCOL):
        lead = work[:, i : i + 1]
        root = 1.0 / jnp.sqrt(work[i : i + 1, i : i + 1])
        line = work[i : i + 1, :] * root
        work = jnp.where(row == i, line, jnp.where(row > i, work - (lead * root) * line, work))
    r_ref[...] = jnp.where(row <= col, work, 0.0)[:, :NCOL]
    for i in range(NCOL):
        lifted = work[:, NCOL + i : NCOL + i + 1] * across[:, i : i + 1]
        c_ref[i] = jnp.broadcast_to(lifted, (NCOL, NT))


def basis_kernel(slabs, gram_ref, right_ref, y_ref, q_ref, r_ref, c_ref):
    @pl.when(pl.program_id(0) == 0)
    def _():
        factor(gram_ref, r_ref, c_ref)

    def step(t, carry):
        a = t // slabs
        here = pl.ds(pl.multiple_of((t % slabs) * LR, LR), LR)
        values = [right_ref[a, r, here, :] for r in range(NRHS)]
        for k in range(POWERS):
            values += [y_ref[k, a, r, here, :] for r in range(NRHS)]
        for j in range(NCOL):
            total = c_ref[0, j : j + 1, :] * values[0]
            for i in range(1, j + 1):
                total = total + c_ref[i, j : j + 1, :] * values[i]
            q_ref[a, j, here, :] = total
        return carry

    lax.fori_loop(0, NV * slabs, step, 0)


def basis(gram, right, ys):
    slabs = 2
    rows = slabs * LR
    f32 = jnp.float32
    return pl.pallas_call(
        functools.partial(basis_kernel, slabs),
        grid=(LS // slabs,),
        out_shape=(
            jax.ShapeDtypeStruct((NV, NCOL, ROWS, NT), f32),
            jax.ShapeDtypeStruct((NCOL, NCOL), f32),
        ),
        in_specs=[
            pl.BlockSpec((NCOL, NT), lambda s: (0, 0)),
            pl.BlockSpec((NV, NRHS, rows, NT), lambda s: (0, 0, s, 0)),
            pl.BlockSpec((POWERS, NV, NRHS, rows, NT), lambda s: (0, 0, 0, s, 0)),
        ],
        out_specs=(
            pl.BlockSpec((NV, NCOL, rows, NT), lambda s: (0, 0, s, 0)),
            pl.BlockSpec((NCOL, NCOL), lambda s: (0, 0)),
        ),
        scratch_shapes=[pltpu.VMEM((NCOL, NCOL, NT), f32)],
    )(gram, right, ys)


def body(n_stream, n_radial, right_side, diag_block, face_coef, jacobians):
    right = right_side.reshape(NV, NRHS, ROWS, NT)
    diag = diag_block.reshape(NV, NV, ROWS, NT)
    face = face_coef.reshape(6, ROWS, NT)
    ys, gram = krylov(n_stream, n_radial, right, diag, face, jacobians)
    q, r_factor = basis(gram, right, ys)
    return q.reshape(NV, NCOL, LS, LR, NT), r_factor


def solution(mesh):
    return jax.shard_map(
        functools.partial(body, mesh.shape["stream"], mesh.shape["radial"]),
        mesh=mesh,
        in_specs=(
            P(None, None, "stream", "radial", None),
            P(None, None, "stream", "radial", None),
            P(None, "stream", "radial", None),
            P(),
        ),
        out_specs=(P(None, None, "stream", "radial", None), P()),
        check_vma=False,
    )
```

time: 953 us -> 67.1 us (0.07)
  blocking collectives: 325 us -> 0 us
  other arithmetic: 320 us -> 0 us
  matrix products: 188 us -> 0 us
  local copies, waits for them, and re-layouts: 66.2 us -> 1.34 us
  Pallas kernels: 0 us -> 64.6 us
  starting transfers between devices: 33.7 us -> 0 us
  between operations: 12.1 us -> 0.64 us
    psum x5 -> x0, blocking collectives: 325 us -> none  [the longest x4 263 us: unit_columns(): lax.psum(jnp.sum(vector * vector, axis=(0, 2, 3, 4)), ('stream', 'radial'))]
    dot_general x20 -> x0, matrix products: 188 us -> none  [the longest x18 137 us: operate(): jnp.einsum('ab,brxyz->arxyz', jacobians[direction], beside_list[direction...]
    div x5 -> x0, other arithmetic: 129 us -> none  [the longest x2 124 us: upper_inverse(): solved[row_number] = pending / factor[row_number, row_number]]
    sub x15 -> x0, other arithmetic: 75.1 us -> none  [upper_factor(): pending - factor_rows[prior_row][row_number] * factor_rows[prior_row]]
    select_n x16 -> x0, other arithmetic: 74.6 us -> none  [upper_factor(): jnp.where(positions >= row_number, pending / pivot_root, jnp.zeros_like(p...]
    pallas_call x0 -> x2, Pallas kernels: none -> 64.6 us  [the longest x1 50.7 us: krylov(): pl.pallas_call(functools.partial(krylov_kernel, n_stream, n_radial), out_...]
    slice x55 -> x0, local copies, waits for them, and re-layouts: 48 us -> none  [the longest x6 10.3 us: operate(): jnp.roll(centre, 1, axis=4)]
    another operation x6 -> x0, other arithmetic: 39 us -> none  [the longest x5 19.6 us: body(): stacked_cols = jnp.stack(columns, axis=1)]
  transfers between devices with their start and end apart: 12 -> 0, of which waited for: 0 -> 0; matrix products, arithmetic and copies ran while one was open for 10% -> 0% of each run, Pallas kernels for 0% -> 0%
where the time goes in v1:
time: 67.1 us; the launch traced here: 66.6 us
  Pallas kernels  64.6 us (96%)
  local copies, waits for them, and re-layouts  1.34 us (2%)
    pallas_call x1, Pallas kernels, krylov(): pl.pallas_call(functools.partial(krylov_kernel, n_stream, n_radial), out_...  50.7 us
    pallas_call x1, Pallas kernels, basis(): pl.pallas_call(functools.partial(basis_kernel, slabs), grid=(LS // slabs,...  14 us

profile of v1, /device:TPU:1, one launch (start us, length us, event | category | flops | bytes accessed | tf_op | source)
XLA Modules:
  0.0 66.6 jit_solution(12191111348141949397)
XLA Ops:
  0.6 1.3 %copy.6.jac_ref = f32[6,5,5]{2,1,0:T(8,128)} copy(f32[6,5,5]{2,0,1:T(8,128)} %param.7) | data formatting | bytes 1200 | tf_op args[3]
  2.0 50.7 %shard_map.59 = (f32[3,5,4,256,128]{4,3,2,1,0:T(8,128)}, f32[16,128]{1,0:T(8,128)}) custom-call(f32[5,4,256,128]{3,2,1,0:T(8,128)} %bitcast.4, f32[5,5,256,128]{3,2,1,0:T(8,128)} %bitcast.6, f32[6,256,128]{2,1,0:T(8,128)} %bitcast.7, f32[6,5,5]{2,1,0:T(8,128)} %copy.6.jac_ref), custom_call_target="tpu_custom_call" | custom-call | tf_op jit(solution)/shard_map/pallas_call | solution.py:366
  52.6 14.0 %shard_map.60 = (f32[5,16,256,128]{3,2,1,0:T(8,128)}, f32[16,16]{1,0:T(8,128)}) custom-call(f32[16,128]{1,0:T(8,128)} %get-tuple-element.6.gram_ref, f32[5,4,256,128]{3,2,1,0:T(8,128)} %bitcast.5, f32[3,5,4,256,128]{4,3,2,1,0:T(8,128)} %get-tuple-element.7.y_ref), custom_call_target="tpu_custom_call" | custom-call | tf_op jit(solution)/shard_map/pallas_call | solution.py:448

commit v2 on v1

--- a/solution.py
+++ b/solution.py
@@ -18,13 +18,15 @@
 SHIFT = 6.0
 BLK = NV * LR
 KDIM = 256
-DIRS = ((0, 0), (1, 0), (2, -1), (3, 1), (4, 0), (5, 0), (2, 0), (3, 0))
+OFFSETS = (0, 0, -1, 1, 0, 0)
+UNROLL = 4
+GRAM_UNROLL = 2
 RAISE = 2.0**24
 MESH = pl.DeviceIdType.MESH
 HIGH = lax.Precision.HIGHEST
 
 
-def build_operator(jac_ref, w_ref):
+def build_operator(jac_ref, w_ref, halo_w_ref):
     col = lax.broadcasted_iota(jnp.int32, (LR, KDIM), 1)
     row = lax.broadcasted_iota(jnp.int32, (LR, KDIM), 0)
     part = col // BLK
@@ -34,93 +36,128 @@
     for offset in (-1, 0, 1):
         hit = (cell == row + offset) & (part < 3)
         masks[offset] = [
-            jnp.where(hit & (var == b), 1.0, 0.0).astype(jnp.float32) for b in range(NV)
+            jnp.where(hit & (var == b), -1.0, 0.0).astype(jnp.float32) for b in range(NV)
         ]
-    for block, (direction, offset) in enumerate(DIRS):
-        for a in range(NV):
-            total = jac_ref[direction, a, 0] * masks[offset][0]
-            for b in range(1, NV):
-                total = total + jac_ref[direction, a, b] * masks[offset][b]
-            head = total.astype(jnp.bfloat16).astype(jnp.float32)
-            mixed = jnp.where(part == 1, total - head, head)
-            start = block * BLK + a * LR
-            w_ref[start : start + LR, :] = mixed.astype(jnp.bfloat16)
-
-
-def split_fields(values, x_ref):
+
+    def tile(direction, a, offset):
+        total = jac_ref[direction, a, 0] * masks[offset][0]
+        for b in range(1, NV):
+            total = total + jac_ref[direction, a, b] * masks[offset][b]
+        head = total.astype(jnp.bfloat16).astype(jnp.float32)
+        return jnp.where(part == 1, total - head, head).astype(jnp.bfloat16)
+
+    for a in range(NV):
+        for direction, offset in enumerate(OFFSETS):
+            start = (a * 6 + direction) * LR
+            w_ref[start : start + LR, :] = tile(direction, a, offset)
+        for direction in range(4):
+            start = direction * BLK + a * LR
+            halo_w_ref[start : start + LR, :] = tile(direction, a, 0)
+
+
+def split_fields(values):
     head = values.astype(jnp.bfloat16)
     tail = (values - head.astype(jnp.float32)).astype(jnp.bfloat16)
+    empty = jnp.zeros((KDIM - 3 * BLK, NT), jnp.bfloat16)
+    columns = []
     for r in range(NRHS):
-        lanes = slice(r * NT, (r + 1) * NT)
         head_r = head[:, r].reshape(BLK, NT)
-        x_ref[0:BLK, lanes] = head_r
-        x_ref[BLK : 2 * BLK, lanes] = head_r
-        x_ref[2 * BLK : 3 * BLK, lanes] = tail[:, r].reshape(BLK, NT)
-
-
-def piece(product, block, r):
-    return product[block * BLK : (block + 1) * BLK, r * NT : (r + 1) * NT].reshape(NV, LR, NT)
-
-
-def apply_inner(source, target, diag_ref, face_ref, w_ref, x_ref, q_ref, scale):
-    target[:, :, 0:LR, :] = jnp.zeros((NV, NRHS, LR, NT), jnp.float32)
-    target[:, :, ROWS : ROWS + LR, :] = jnp.zeros((NV, NRHS, LR, NT), jnp.float32)
-
-    def step(s, carry):
-        here = pl.ds(pl.multiple_of(s * LR, LR), LR)
-        after = pl.ds(pl.multiple_of((s + 1) * LR, LR), LR)
-        before = pl.ds(pl.multiple_of(((s + LS) % (LS + 1)) * LR, LR), LR)
-        face_after = pl.ds(pl.multiple_of(jnp.minimum(s + 1, LS - 1) * LR, LR), LR)
-        face_before = pl.ds(pl.multiple_of(jnp.maximum(s - 1, 0) * LR, LR), LR)
-        values = source[:, :, here, :]
-        split_fields(values, x_ref)
-        q_ref[...] = jnp.dot(w_ref[0 : 6 * BLK, :], x_ref[...], preferred_element_type=jnp.float32)
-        f0 = face_ref[0, face_after, :] * scale
-        f1 = face_ref[1, face_before, :] * scale
-        f2, f3, f4, f5 = (face_ref[d, here, :] for d in range(2, 6))
-        for r in range(NRHS):
-            mine = values[:, r]
-            total = -SHIFT * mine
+        tail_r = tail[:, r].reshape(BLK, NT)
+        columns.append(jnp.concatenate([head_r, head_r, tail_r, empty], axis=0))
+    return jnp.concatenate(columns, axis=1)
+
+
+def slab(s):
+    return pl.ds(pl.multiple_of(s * LR, LR), LR)
+
+
+def apply_blocks(source, diag_ref, stage, s, scale):
+    for half in range(2):
+        rows = pl.ds(pl.multiple_of(s * LR + half * 8, 8), 8)
+        fields = [[source[b, r, rows, :] for r in range(NRHS)] for b in range(NV)]
+        for a in range(NV):
+            totals = [None] * NRHS
             for b in range(NV):
-                total = total + diag_ref[:, b, here, :] * mine[b]
-            total = total - f2 * piece(q_ref, 2, r)
-            total = total - f3 * piece(q_ref, 3, r)
-            total = total - f4 * pltpu.roll(piece(q_ref, 4, r), 1, 2)
-            total = total - f5 * pltpu.roll(piece(q_ref, 5, r), NT - 1, 2)
+                block = diag_ref[a, b, rows, :]
+                if scale != 1.0:
+                    block = block * scale
+                for r in range(NRHS):
+                    term = block * fields[b][r]
+                    totals[r] = term if b == 0 else totals[r] + term
+            for r in range(NRHS):
+                stage[a, r, half * 8 : half * 8 + 8, :] = totals[r]
+
+
+def apply_inner(source, target, diag_ref, face_ref, w_ref, stages, ahead_ref, open_ref, scale):
+    cells = [(a, r) for a in range(NV) for r in range(NRHS)]
+    ahead_ref[...] = jnp.zeros((NV, NRHS, LR, NT), jnp.float32)
+    open_ref[...] = jnp.zeros((NV, NRHS, LR, NT), jnp.float32)
+
+    def step(t, carry):
+        s0 = t * UNROLL
+        for u in range(UNROLL):
+            apply_blocks(source, diag_ref, stages[u], s0 + u, scale)
+        ahead = {cell: ahead_ref[cell[0], cell[1]] for cell in cells}
+        unfinished = {cell: open_ref[cell[0], cell[1]] for cell in cells}
+        for u in range(UNROLL):
+            s = s0 + u
+            before = jnp.where(s == 0, LS, s - 1) if u == 0 else s - 1
+            product = jnp.dot(
+                w_ref[...],
+                split_fields(source[:, :, slab(s), :]),
+                preferred_element_type=jnp.float32,
+            )
+            face = [face_ref[0, slab(jnp.minimum(s + 1, LS - 1)), :]]
+            face.append(face_ref[1, slab(jnp.maximum(s - 1, 0)), :])
+            face += [face_ref[d, slab(s), :] for d in range(2, 6)]
             if scale != 1.0:
-                total = total * scale
-            target[:, r, here, :] = target[:, r, here, :] + total
-            target[:, r, after, :] = -(f0 * piece(q_ref, 0, r))
-            target[:, r, before, :] = target[:, r, before, :] - f1 * piece(q_ref, 1, r)
+                face = [weight * scale for weight in face]
+            for a, r in cells:
+
+                def part(d, a=a, r=r):
+                    start = (a * 6 + d) * LR
+                    return product[start : start + LR, r * NT : (r + 1) * NT]
+
+                target[a, r, slab(before), :] = unfinished[a, r] + face[1] * part(1)
+                total = face[2] * part(2) + face[3] * part(3)
+                total = total + face[4] * pltpu.roll(part(4), 1, 1)
+                total = total + face[5] * pltpu.roll(part(5), NT - 1, 1)
+                unfinished[a, r] = total + (stages[u][a, r] + ahead[a, r])
+                ahead[a, r] = face[0] * part(0)
+        for a, r in cells:
+            ahead_ref[a, r] = ahead[a, r]
+            open_ref[a, r] = unfinished[a, r]
         return carry
 
-    lax.fori_loop(0, LS, step, 0)
-
-
-def add_halo(target, face_ref, w_ref, x_ref, slabs, edges, rows_ref, scale):
+    lax.fori_loop(0, LS // UNROLL, step, 0)
+    target[:, :, ROWS - LR : ROWS, :] = open_ref[...]
+
+
+def add_halo(target, face_ref, halo_w_ref, slabs, edges, rows_ref, scale):
     for side in range(2):
         start = 0 if side == 0 else ROWS - LR
-        split_fields(slabs[side], x_ref)
         product = jnp.dot(
-            w_ref[side * BLK : (side + 1) * BLK, :], x_ref[...], preferred_element_type=jnp.float32
+            halo_w_ref[side * BLK : (side + 1) * BLK, :],
+            split_fields(slabs[side]),
+            preferred_element_type=jnp.float32,
         )
         weight = face_ref[side, start : start + LR, :] * scale
-        for r in range(NRHS):
-            target[:, r, start : start + LR, :] = target[
-                :, r, start : start + LR, :
-            ] - weight * piece(product, 0, r)
+        for a in range(NV):
+            for r in range(NRHS):
+                target[a, r, start : start + LR, :] = target[a, r, start : start + LR, :] + (
+                    weight * product[a * LR : (a + 1) * LR, r * NT : (r + 1) * NT]
+                )
     for side in range(2):
         rows = pl.ds(0 if side == 0 else LR - 1, LS, stride=LR)
-        split_fields(edges[side], x_ref)
         product = jnp.dot(
-            w_ref[(6 + side) * BLK : (7 + side) * BLK, :],
-            x_ref[...],
+            halo_w_ref[(2 + side) * BLK : (3 + side) * BLK, :],
+            split_fields(edges[side]),
             preferred_element_type=jnp.float32,
         )
         weight = face_ref[2 + side, rows, :] * scale
         for a in range(NV):
             for r in range(NRHS):
-                fresh = target[a, r, rows, :] - weight * (
+                fresh = target[a, r, rows, :] + weight * (
                     product[a * LR : (a + 1) * LR, r * NT : (r + 1) * NT]
                 )
                 target[a, r, rows, :] = fresh
@@ -128,16 +165,18 @@
                     rows_ref[side, a, r] = fresh
 
 
-def local_gram(y_ref, m_ref):
+def local_gram(ys, m_ref):
     m_ref[...] = jnp.zeros((ROWS, ROWS), jnp.float32)
 
-    def step(s, carry):
-        here = pl.ds(pl.multiple_of(s * LR, LR), LR)
+    def step(t, carry):
         left = []
         right = []
-        for a in range(NV):
+        for u in range(GRAM_UNROLL * NV):
+            s = t * GRAM_UNROLL + u // NV
+            a = u % NV
+            here = pl.ds(pl.multiple_of(s * LR, LR), LR)
             values = jnp.concatenate(
-                [y_ref[k, a, :, here, :].reshape(NRHS * LR, NT) for k in range(POWERS + 1)], axis=0
+                [y_ref[a, :, here, :].reshape(NRHS * LR, NT) for y_ref in ys], axis=0
             )
             head = values.astype(jnp.bfloat16)
             tail = (2.0 * (values - head.astype(jnp.float32))).astype(jnp.bfloat16)
@@ -151,7 +190,7 @@
         )
         return carry
 
-    lax.fori_loop(0, LS, step, 0)
+    lax.fori_loop(0, LS // GRAM_UNROLL, step, 0)
     row = lax.broadcasted_iota(jnp.int32, (ROWS, ROWS), 0)
     col = lax.broadcasted_iota(jnp.int32, (ROWS, ROWS), 1)
     kept = jnp.where(row % LR == col % LR, m_ref[...], 0.0)
@@ -173,15 +212,24 @@
     right_hbm,
     diag_hbm,
     face_hbm,
-    jac_ref,
+    jac_hbm,
     y_hbm,
     gram_ref,
-    y_ref,
+    y0_ref,
+    y1_ref,
+    y2_ref,
+    y3_ref,
     diag_ref,
     face_ref,
+    jac_ref,
     w_ref,
-    x_ref,
-    q_ref,
+    halo_w_ref,
+    stage0_ref,
+    stage1_ref,
+    stage2_ref,
+    stage3_ref,
+    ahead_ref,
+    open_ref,
     slab_ref,
     edge_ref,
     pack_ref,
@@ -197,6 +245,8 @@
     second_send,
     second_recv,
 ):
+    ys = (y0_ref, y1_ref, y2_ref, y3_ref)
+    stages = (stage0_ref, stage1_ref, stage2_ref, stage3_ref)
     si = lax.axis_index("stream")
     ri = lax.axis_index("radial")
     core = si % 2
@@ -213,9 +263,10 @@
         return (((chip + offset) % n_second) * 2 + core, ri)
 
     loads = [
-        pltpu.make_async_copy(right_hbm, y_ref.at[0, :, :, pl.ds(0, ROWS), :], load_sem.at[0]),
+        pltpu.make_async_copy(right_hbm, y0_ref.at[:, :, pl.ds(0, ROWS), :], load_sem.at[0]),
         pltpu.make_async_copy(face_hbm, face_ref, load_sem.at[1]),
         pltpu.make_async_copy(diag_hbm, diag_ref, load_sem.at[2]),
+        pltpu.make_async_copy(jac_hbm, jac_ref, load_sem.at[3]),
     ]
     for load in loads:
         load.start()
@@ -234,8 +285,8 @@
         def _(j=j):
             pl.semaphore_signal(barrier, inc=1, device_id=peers[j], device_id_type=MESH)
 
-    x_ref[3 * BLK :, :] = jnp.zeros((KDIM - 3 * BLK, NRHS * NT), jnp.bfloat16)
-    build_operator(jac_ref, w_ref)
+    loads[3].wait()
+    build_operator(jac_ref, w_ref, halo_w_ref)
     for side in range(2):
 
         @pl.when(jnp.logical_not(present[1 - side]))
@@ -254,7 +305,7 @@
     def halo_copy(k, j):
         if j < 2:
             start = ROWS - LR if j == 0 else 0
-            whole = right_hbm if k == 0 else y_ref.at[k]
+            whole = right_hbm if k == 0 else ys[k]
             src = whole.at[:, :, pl.ds(start, LR), :]
             dst = slab_ref.at[k, j]
         else:
@@ -289,23 +340,26 @@
         rows = pl.ds(0 if side == 0 else LR - 1, LS, stride=LR)
         for a in range(NV):
             for r in range(NRHS):
-                pack_ref[0, side, a, r] = y_ref[0, a, r, rows, :]
+                pack_ref[0, side, a, r] = y0_ref[a, r, rows, :]
     send_halo(0, (2, 3))
     loads[1].wait()
     loads[2].wait()
+    for a in range(NV):
+        diag_ref[a, a] = diag_ref[a, a] - SHIFT
 
     stores = []
     for k in range(POWERS):
         scale = RAISE if k == 0 else 1.0
-        target = y_ref.at[k + 1]
-        apply_inner(y_ref.at[k], target, diag_ref, face_ref, w_ref, x_ref, q_ref, scale)
+        target = ys[k + 1]
+        apply_inner(
+            ys[k], target, diag_ref, face_ref, w_ref, stages, ahead_ref, open_ref, scale
+        )
         wait_halo(k)
         last = k == POWERS - 1
         add_halo(
             target,
             face_ref,
-            w_ref,
-            x_ref,
+            halo_w_ref,
             (slab_ref[k, 0], slab_ref[k, 1]),
             (edge_ref[k, 0], edge_ref[k, 1]),
             None if last else pack_ref.at[k + 1],
@@ -342,7 +396,7 @@
             total = total + slots[index]
         return total
 
-    gram = local_gram(y_ref, m_ref)
+    gram = local_gram(ys, m_ref)
     gram = reduce_over(gram, first_ref, first_send, first_recv, n_first, me_first, first_peer)
     gram = reduce_over(gram, second_ref, second_send, second_recv, n_second, chip, second_peer)
     gram_ref[...] = gram
@@ -369,22 +423,31 @@
             jax.ShapeDtypeStruct((POWERS, NV, NRHS, ROWS, NT), f32),
             jax.ShapeDtypeStruct((NCOL, NT), f32),
         ),
-        in_specs=[any_spec, any_spec, any_spec, pl.BlockSpec(memory_space=pltpu.SMEM)],
+        in_specs=[any_spec, any_spec, any_spec, any_spec],
         out_specs=(any_spec, pl.BlockSpec(memory_space=pltpu.VMEM)),
         scratch_shapes=[
-            pltpu.VMEM((POWERS + 1, NV, NRHS, ROWS + LR, NT), f32),
+            pltpu.VMEM((NV, NRHS, ROWS + LR, NT), f32),
+            pltpu.VMEM((NV, NRHS, ROWS + LR, NT), f32),
+            pltpu.VMEM((NV, NRHS, ROWS + LR, NT), f32),
+            pltpu.VMEM((NV, NRHS, ROWS + LR, NT), f32),
             pltpu.VMEM((NV, NV, ROWS, NT), f32),
             pltpu.VMEM((6, ROWS, NT), f32),
-            pltpu.VMEM((len(DIRS) * BLK, KDIM), jnp.bfloat16),
-            pltpu.VMEM((KDIM, NRHS * NT), jnp.bfloat16),
-            pltpu.VMEM((6 * BLK, NRHS * NT), f32),
+            pltpu.SMEM((6, NV, NV), f32),
+            pltpu.VMEM((6 * BLK, KDIM), jnp.bfloat16),
+            pltpu.VMEM((4 * BLK, KDIM), jnp.bfloat16),
+            pltpu.VMEM((NV, NRHS, LR, NT), f32),
+            pltpu.VMEM((NV, NRHS, LR, NT), f32),
+            pltpu.VMEM((NV, NRHS, LR, NT), f32),
+            pltpu.VMEM((NV, NRHS, LR, NT), f32),
+            pltpu.VMEM((NV, NRHS, LR, NT), f32),
+            pltpu.VMEM((NV, NRHS, LR, NT), f32),
             pltpu.VMEM((POWERS, 2, NV, NRHS, LR, NT), f32),
             pltpu.VMEM((POWERS, 2, NV, NRHS, LS, NT), f32),
             pltpu.VMEM((POWERS, 2, NV, NRHS, LS, NT), f32),
             pltpu.VMEM((ROWS, ROWS), f32),
             pltpu.VMEM((n_first, NCOL, NT), f32),
             pltpu.VMEM((n_second, NCOL, NT), f32),
-            dma((3,)),
+            dma((4,)),
             dma((POWERS,)),
             dma((POWERS, 4)),
             dma((POWERS, 4)),

time: 67.1 us -> 56.7 us (0.85)
  Pallas kernels: 64.6 us -> 54.3 us
    pallas_call x1, Pallas kernels: 50.7 us -> 40.4 us  [krylov(): pl.pallas_call(functools.partial(krylov_kernel, n_stream, n_radial), out_...]
where the time goes in v2:
time: 56.7 us; the launch traced here: 56.3 us
  Pallas kernels  54.3 us (96%)
  local copies, waits for them, and re-layouts  1.34 us (2%)
  between operations  0.64 us (1%)
    pallas_call x1, Pallas kernels, krylov(): pl.pallas_call(functools.partial(krylov_kernel, n_stream, n_radial), out_...  40.4 us
    pallas_call x1, Pallas kernels, basis(): pl.pallas_call(functools.partial(basis_kernel, slabs), grid=(LS // slabs,...  14 us
    unnamed x1, local copies, waits for them, and re-layouts  1.34 us

profile of v2, /device:TPU:1, one launch (start us, length us, event | category | flops | bytes accessed | tf_op | source)
XLA Modules:
  0.0 56.3 jit_solution(3277965728624469306)
XLA Ops:
  0.6 1.3 %copy.6.jac_hbm = f32[6,5,5]{2,1,0:T(8,128)} copy(f32[6,5,5]{2,0,1:T(8,128)} %param.7) | data formatting | bytes 1200 | tf_op args[3]
  2.0 40.4 %shard_map.59 = (f32[3,5,4,256,128]{4,3,2,1,0:T(8,128)}, f32[16,128]{1,0:T(8,128)}) custom-call(f32[5,4,256,128]{3,2,1,0:T(8,128)} %bitcast.4, f32[5,5,256,128]{3,2,1,0:T(8,128)} %bitcast.6, f32[6,256,128]{2,1,0:T(8,128)} %bitcast.7, f32[6,5,5]{2,1,0:T(8,128)} %copy.6.jac_hbm), custom_call_target="tpu_custom_call" | custom-call | tf_op jit(solution)/shard_map/pallas_call | solution.py:420
  42.3 14.0 %shard_map.60 = (f32[5,16,256,128]{3,2,1,0:T(8,128)}, f32[16,16]{1,0:T(8,128)}) custom-call(f32[16,128]{1,0:T(8,128)} %get-tuple-element.6.gram_ref, f32[5,4,256,128]{3,2,1,0:T(8,128)} %bitcast.5, f32[3,5,4,256,128]{4,3,2,1,0:T(8,128)} %get-tuple-element.7.y_ref), custom_call_target="tpu_custom_call" | custom-call | tf_op jit(solution)/shard_map/pallas_call | solution.py:511

commit v3 on v2

--- a/solution.py
+++ b/solution.py
@@ -21,6 +21,8 @@
 OFFSETS = (0, 0, -1, 1, 0, 0)
 UNROLL = 4
 GRAM_UNROLL = 2
+BASIS_SLABS = 2
+HALF = 8
 RAISE = 2.0**24
 MESH = pl.DeviceIdType.MESH
 HIGH = lax.Precision.HIGHEST
@@ -40,9 +42,9 @@
         ]
 
     def tile(direction, a, offset):
-        total = jac_ref[direction, a, 0] * masks[offset][0]
+        total = jac_ref[a, direction, 0] * masks[offset][0]
         for b in range(1, NV):
-            total = total + jac_ref[direction, a, b] * masks[offset][b]
+            total = total + jac_ref[a, direction, b] * masks[offset][b]
         head = total.astype(jnp.bfloat16).astype(jnp.float32)
         return jnp.where(part == 1, total - head, head).astype(jnp.bfloat16)
 
@@ -213,12 +215,11 @@
     diag_hbm,
     face_hbm,
     jac_hbm,
-    y_hbm,
-    gram_ref,
     y0_ref,
     y1_ref,
     y2_ref,
     y3_ref,
+    gram_ref,
     diag_ref,
     face_ref,
     jac_ref,
@@ -237,7 +238,6 @@
     first_ref,
     second_ref,
     load_sem,
-    out_sem,
     halo_send,
     halo_recv,
     first_send,
@@ -347,7 +347,6 @@
     for a in range(NV):
         diag_ref[a, a] = diag_ref[a, a] - SHIFT
 
-    stores = []
     for k in range(POWERS):
         scale = RAISE if k == 0 else 1.0
         target = ys[k + 1]
@@ -367,11 +366,6 @@
         )
         if not last:
             send_halo(k + 1, range(4))
-        store = pltpu.make_async_copy(
-            target.at[:, :, pl.ds(0, ROWS), :], y_hbm.at[k], out_sem.at[k]
-        )
-        store.start()
-        stores.append(store)
 
     def reduce_over(value, slots, send, recv, count, me, peer):
         slots[me] = value
@@ -407,12 +401,9 @@
             def _(k=k, j=j):
                 halo_copy(k, j).wait_send()
 
-    for store in stores:
-        store.wait()
-
 
 def krylov(n_stream, n_radial, right, diag, face, jac):
-    any_spec = pl.BlockSpec(memory_space=pl.ANY)
+    hbm = pl.BlockSpec(memory_space=pltpu.HBM)
     f32 = jnp.float32
     dma = pltpu.SemaphoreType.DMA
     n_first = 2 * n_radial
@@ -420,19 +411,15 @@
     return pl.pallas_call(
         functools.partial(krylov_kernel, n_stream, n_radial),
         out_shape=(
-            jax.ShapeDtypeStruct((POWERS, NV, NRHS, ROWS, NT), f32),
+            *[pltpu.VMEM((NV, NRHS, ROWS + LR, NT), f32)] * (POWERS + 1),
             jax.ShapeDtypeStruct((NCOL, NT), f32),
         ),
-        in_specs=[any_spec, any_spec, any_spec, any_spec],
-        out_specs=(any_spec, pl.BlockSpec(memory_space=pltpu.VMEM)),
+        in_specs=[hbm] * 4,
+        out_specs=tuple([pl.BlockSpec(memory_space=pltpu.VMEM)] * (POWERS + 2)),
         scratch_shapes=[
-            pltpu.VMEM((NV, NRHS, ROWS + LR, NT), f32),
-            pltpu.VMEM((NV, NRHS, ROWS + LR, NT), f32),
-            pltpu.VMEM((NV, NRHS, ROWS + LR, NT), f32),
-            pltpu.VMEM((NV, NRHS, ROWS + LR, NT), f32),
             pltpu.VMEM((NV, NV, ROWS, NT), f32),
             pltpu.VMEM((6, ROWS, NT), f32),
-            pltpu.SMEM((6, NV, NV), f32),
+            pltpu.SMEM((NV, 6, NV), f32),
             pltpu.VMEM((6 * BLK, KDIM), jnp.bfloat16),
             pltpu.VMEM((4 * BLK, KDIM), jnp.bfloat16),
             pltpu.VMEM((NV, NRHS, LR, NT), f32),
@@ -448,7 +435,6 @@
             pltpu.VMEM((n_first, NCOL, NT), f32),
             pltpu.VMEM((n_second, NCOL, NT), f32),
             dma((4,)),
-            dma((POWERS,)),
             dma((POWERS, 4)),
             dma((POWERS, 4)),
             dma((n_first,)),
@@ -456,7 +442,7 @@
             dma((n_second,)),
             dma((n_second,)),
         ],
-        compiler_params=pltpu.CompilerParams(collective_id=0, has_side_effects=True),
+        compiler_params=pltpu.CompilerParams(collective_id=0, has_side_effects=True, vmem_limit_bytes=55_500_000),
     )(right, diag, face, jac)
 
 
@@ -478,36 +464,62 @@
         line = work[i : i + 1, :] * root
         work = jnp.where(row == i, line, jnp.where(row > i, work - (lead * root) * line, work))
     r_ref[...] = jnp.where(row <= col, work, 0.0)[:, :NCOL]
-    for i in range(NCOL):
-        lifted = work[:, NCOL + i : NCOL + i + 1] * across[:, i : i + 1]
-        c_ref[i] = jnp.broadcast_to(lifted, (NCOL, NT))
-
-
-def basis_kernel(slabs, gram_ref, right_ref, y_ref, q_ref, r_ref, c_ref):
+    wide = NCOL * HALF
+    col_of = lax.broadcasted_iota(jnp.int32, (NCOL, wide), 1)
+    row_of = lax.broadcasted_iota(jnp.int32, (NCOL, wide), 0)
+    spread = jnp.where(col_of // HALF == row_of, down, 0.0)
+    repeat_row = lax.broadcasted_iota(jnp.int32, (wide, NCOL), 0)
+    repeat_col = lax.broadcasted_iota(jnp.int32, (wide, NCOL), 1)
+    repeat = jnp.where(repeat_row // HALF == repeat_col, 1.0, 0.0).astype(jnp.float32)
+    lifted = jnp.dot(
+        work[:, NCOL : 2 * NCOL], spread, precision=HIGH, preferred_element_type=jnp.float32
+    )
+    lifted = jnp.dot(repeat, lifted, precision=HIGH, preferred_element_type=jnp.float32)
+    full_row = lax.broadcasted_iota(jnp.int32, (wide, wide), 0)
+    full_col = lax.broadcasted_iota(jnp.int32, (wide, wide), 1)
+    lifted = jnp.where(full_row % HALF == full_col % HALF, lifted, 0.0)
+    head = lifted.astype(jnp.bfloat16)
+    tail = (lifted - head.astype(jnp.float32)).astype(jnp.bfloat16)
+    c_ref[...] = jnp.concatenate([head, head, tail], axis=1)
+
+
+def basis_kernel(slabs, gram_ref, y0_ref, y1_ref, y2_ref, y3_ref, q_ref, r_ref, c_ref):
     @pl.when(pl.program_id(0) == 0)
     def _():
         factor(gram_ref, r_ref, c_ref)
 
-    def step(t, carry):
-        a = t // slabs
-        here = pl.ds(pl.multiple_of((t % slabs) * LR, LR), LR)
-        values = [right_ref[a, r, here, :] for r in range(NRHS)]
-        for k in range(POWERS):
-            values += [y_ref[k, a, r, here, :] for r in range(NRHS)]
-        for j in range(NCOL):
-            total = c_ref[0, j : j + 1, :] * values[0]
-            for i in range(1, j + 1):
-                total = total + c_ref[i, j : j + 1, :] * values[i]
-            q_ref[a, j, here, :] = total
+    first = pl.program_id(0) * slabs
+
+    def step(a, carry):
+        for half in range(LR // HALF):
+            columns = []
+            for s in range(slabs):
+                rows = pl.ds(pl.multiple_of((first + s) * LR + half * HALF, HALF), HALF)
+                column = []
+                for y_ref in (y0_ref, y1_ref, y2_ref, y3_ref):
+                    column += [y_ref[a, r, rows, :] for r in range(NRHS)]
+                columns.append(jnp.concatenate(column, axis=0))
+            values = jnp.concatenate(columns, axis=1)
+            head = values.astype(jnp.bfloat16)
+            tail = (values - head.astype(jnp.float32)).astype(jnp.bfloat16)
+            stacked = jnp.concatenate([head, tail, head], axis=0)
+            product = jnp.dot(c_ref[...], stacked, preferred_element_type=jnp.float32)
+            for s in range(slabs):
+                rows = slice(s * LR + half * HALF, s * LR + (half + 1) * HALF)
+                for j in range(NCOL):
+                    q_ref[a, j, rows, :] = product[
+                        j * HALF : (j + 1) * HALF, s * NT : (s + 1) * NT
+                    ]
         return carry
 
-    lax.fori_loop(0, NV * slabs, step, 0)
-
-
-def basis(gram, right, ys):
-    slabs = 2
+    lax.fori_loop(0, NV, step, 0)
+
+
+def basis(gram, fields):
+    slabs = BASIS_SLABS
     rows = slabs * LR
     f32 = jnp.float32
+    vmem = pl.BlockSpec(memory_space=pltpu.VMEM)
     return pl.pallas_call(
         functools.partial(basis_kernel, slabs),
         grid=(LS // slabs,),
@@ -515,25 +527,23 @@
             jax.ShapeDtypeStruct((NV, NCOL, ROWS, NT), f32),
             jax.ShapeDtypeStruct((NCOL, NCOL), f32),
         ),
-        in_specs=[
-            pl.BlockSpec((NCOL, NT), lambda s: (0, 0)),
-            pl.BlockSpec((NV, NRHS, rows, NT), lambda s: (0, 0, s, 0)),
-            pl.BlockSpec((POWERS, NV, NRHS, rows, NT), lambda s: (0, 0, 0, s, 0)),
-        ],
+        in_specs=[vmem] * (POWERS + 2),
         out_specs=(
             pl.BlockSpec((NV, NCOL, rows, NT), lambda s: (0, 0, s, 0)),
             pl.BlockSpec((NCOL, NCOL), lambda s: (0, 0)),
         ),
-        scratch_shapes=[pltpu.VMEM((NCOL, NCOL, NT), f32)],
-    )(gram, right, ys)
+        scratch_shapes=[pltpu.VMEM((NCOL * HALF, 3 * NCOL * HALF), jnp.bfloat16)],
+        compiler_params=pltpu.CompilerParams(vmem_limit_bytes=30 * 2**20),
+    )(gram, *fields)
 
 
 def body(n_stream, n_radial, right_side, diag_block, face_coef, jacobians):
     right = right_side.reshape(NV, NRHS, ROWS, NT)
     diag = diag_block.reshape(NV, NV, ROWS, NT)
     face = face_coef.reshape(6, ROWS, NT)
-    ys, gram = krylov(n_stream, n_radial, right, diag, face, jacobians)
-    q, r_factor = basis(gram, right, ys)
+    jac = jnp.transpose(jacobians, (1, 0, 2))
+    *fields, gram = krylov(n_stream, n_radial, right, diag, face, jac)
+    q, r_factor = basis(gram, fields)
     return q.reshape(NV, NCOL, LS, LR, NT), r_factor
 
 

time: 56.7 us -> 54.8 us (0.966)
  Pallas kernels: 54.3 us -> 53.2 us
  local copies, waits for them, and re-layouts: 1.34 us -> 0.69 us
    pallas_call x1, Pallas kernels: 14 us -> 12.6 us  [basis(): pl.pallas_call(functools.partial(basis_kernel, slabs), grid=(LS // slabs,...]
    unnamed x1 -> x2, local copies, waits for them, and re-layouts: 1.34 us -> 0.69 us
where the time goes in v3:
time: 54.8 us; the launch traced here: 54.6 us
  Pallas kernels  53.2 us (97%)
  local copies, waits for them, and re-layouts  0.69 us (1%)
  between operations  0.65 us (1%)
    pallas_call x1, Pallas kernels, krylov(): pl.pallas_call(functools.partial(krylov_kernel, n_stream, n_radial), out_...  40.6 us
    pallas_call x1, Pallas kernels, basis(): pl.pallas_call(functools.partial(basis_kernel, slabs), grid=(LS // slabs,...  12.6 us

profile of v3, /device:TPU:1, one launch (start us, length us, event | category | flops | bytes accessed | tf_op | source)
XLA Modules:
  0.0 54.6 jit_solution(367912401753103364)
XLA Ops:
  0.6 40.6 %shard_map.59 = (f32[5,4,272,128]{3,2,1,0:T(8,128)S(1)}, f32[5,4,272,128]{3,2,1,0:T(8,128)S(1)}, f32[5,4,272,128]{3,2,1,0:T(8,128)S(1)}, f32[5,4,272,128]{3,2,1,0:T(8,128)S(1)}, f32[16,128]{1,0:T(8,128)}) custom-call(f32[5,4,256,128]{3,2,1,0:T(8,128)} %bitcast.6, f32[5,5,256,128]{3,2,1,0:T(8,128)} %bitcast.5, f32[6,256,128]{2,1,0:T(8,128)} %bitcast.7, ...), custom_call_target="tpu_custom_call" | custom-call | tf_op jit(solution)/shard_map/pallas_call | solution.py:411
  41.2 0.0 copy-start
  41.2 0.7 %copy-done = f32[16,128]{1,0:T(8,128)S(1)} copy-done((f32[16,128]{1,0:T(8,128)S(1)}, f32[16,128]{1,0:T(8,128)}, u32[]{:S(2)}) %copy-start) | copy-done | bytes 8216
  41.9 12.6 %shard_map.60 = (f32[5,16,256,128]{3,2,1,0:T(8,128)}, f32[16,16]{1,0:T(8,128)}) custom-call(f32[16,128]{1,0:T(8,128)S(1)} %copy-done, f32[5,4,272,128]{3,2,1,0:T(8,128)S(1)} %get-tuple-element.10.y0_ref, f32[5,4,272,128]{3,2,1,0:T(8,128)S(1)} %get-tuple-element.11.y1_ref, f32[5,4,272,128]{3,2,1,0:T(8,128)S(1)} %get-tuple-element.12.y2_ref, ...), custom_call_target="tpu_custom_call" | custom-call | tf_op jit(solution)/shard_map/pallas_call | solution.py:523
Async XLA Ops:
  41.2 0.7 %copy-start = (f32[16,128]{1,0:T(8,128)S(1)}, f32[16,128]{1,0:T(8,128)}, u32[]{:S(2)}) copy-start(f32[16,128]{1,0:T(8,128)} %get-tuple-element.9.gram_ref) | copy-start | bytes 24580

commit v4 on v3

--- a/solution.py
+++ b/solution.py
@@ -20,12 +20,11 @@
 KDIM = 256
 OFFSETS = (0, 0, -1, 1, 0, 0)
 UNROLL = 4
-GRAM_UNROLL = 2
-BASIS_SLABS = 2
-HALF = 8
+GRAM_ROWS = 32
+GRAM_CHUNKS = ROWS // GRAM_ROWS
+DONE = 12
 RAISE = 2.0**24
 MESH = pl.DeviceIdType.MESH
-HIGH = lax.Precision.HIGHEST
 
 
 def build_operator(jac_ref, w_ref, halo_w_ref):
@@ -167,45 +166,77 @@
                     rows_ref[side, a, r] = fresh
 
 
-def local_gram(ys, m_ref):
-    m_ref[...] = jnp.zeros((ROWS, ROWS), jnp.float32)
-
-    def step(t, carry):
-        left = []
-        right = []
-        for u in range(GRAM_UNROLL * NV):
-            s = t * GRAM_UNROLL + u // NV
-            a = u % NV
-            here = pl.ds(pl.multiple_of(s * LR, LR), LR)
-            values = jnp.concatenate(
-                [y_ref[a, :, here, :].reshape(NRHS * LR, NT) for y_ref in ys], axis=0
-            )
-            head = values.astype(jnp.bfloat16)
-            tail = (2.0 * (values - head.astype(jnp.float32))).astype(jnp.bfloat16)
-            left += [head, tail]
-            right += [head, head]
-        m_ref[...] += lax.dot_general(
-            jnp.concatenate(left, axis=1),
-            jnp.concatenate(right, axis=1),
-            (((1,), (1,)), ((), ())),
-            preferred_element_type=jnp.float32,
-        )
-        return carry
-
-    lax.fori_loop(0, LS // GRAM_UNROLL, step, 0)
-    row = lax.broadcasted_iota(jnp.int32, (ROWS, ROWS), 0)
-    col = lax.broadcasted_iota(jnp.int32, (ROWS, ROWS), 1)
-    kept = jnp.where(row % LR == col % LR, m_ref[...], 0.0)
-    pick_row = lax.broadcasted_iota(jnp.int32, (NCOL, ROWS), 0)
-    pick_col = lax.broadcasted_iota(jnp.int32, (NCOL, ROWS), 1)
-    pick = jnp.where(pick_col // LR == pick_row, 1.0, 0.0).astype(jnp.float32)
-    wide_row = lax.broadcasted_iota(jnp.int32, (NT, ROWS), 0)
-    wide_col = lax.broadcasted_iota(jnp.int32, (NT, ROWS), 1)
-    wide = jnp.where(wide_col // LR == wide_row, 1.0, 0.0).astype(jnp.float32)
-    half = jnp.dot(pick, kept, precision=HIGH, preferred_element_type=jnp.float32)
-    return lax.dot_general(
-        half, wide, (((1,), (1,)), ((), ())), precision=HIGH, preferred_element_type=jnp.float32
-    )
+def gram_block(left, right, acc_ref, k, j):
+    pairs = [(p, q) for p in range(NRHS) for q in range(NRHS) if k != j or q <= p]
+
+    def step(t, sums):
+        a = t // GRAM_CHUNKS
+        rows = pl.ds(pl.multiple_of((t % GRAM_CHUNKS) * GRAM_ROWS, GRAM_ROWS), GRAM_ROWS)
+        mine = [left[a, p, rows, :] for p in range(NRHS)]
+        other = mine if k == j else [right[a, q, rows, :] for q in range(NRHS)]
+        fresh = []
+        for index, (p, q) in enumerate(pairs):
+            term = mine[p] * other[q]
+            total = sums[index]
+            for piece in range(GRAM_ROWS // 8):
+                total = total + term[piece * 8 : piece * 8 + 8]
+            fresh.append(total)
+        return tuple(fresh)
+
+    empty = tuple(jnp.zeros((8, NT), jnp.float32) for _ in pairs)
+    sums = lax.fori_loop(0, NV * GRAM_CHUNKS, step, empty)
+    for index, (p, q) in enumerate(pairs):
+        acc_ref[4 * k + p, 4 * j + q] = sums[index]
+        if k == j and p != q:
+            acc_ref[4 * k + q, 4 * j + p] = sums[index]
+
+
+def gram_columns(acc_ref, columns):
+    lane = lax.broadcasted_iota(jnp.int32, (NCOL, NT), 1)
+    table = jnp.zeros((NCOL, NT), jnp.float32)
+    for i in columns:
+        rows = jnp.sum(acc_ref[i], axis=1)
+        table = table + jnp.where(lane == i, jnp.sum(rows, axis=1, keepdims=True), 0.0)
+    return table
+
+
+def eliminate(table, count):
+    row = lax.broadcasted_iota(jnp.int32, (NCOL, NT), 0)
+    col = lax.broadcasted_iota(jnp.int32, (NCOL, NT), 1)
+    square = table[:, :NCOL]
+    flipped = jnp.concatenate([square.T, jnp.zeros((NCOL, NT - NCOL), jnp.float32)], axis=1)
+    gram = jnp.where((row // NRHS > col // NRHS) & (col < NCOL), flipped, table)
+    on_diag = jnp.where(row == col, gram, 0.0)
+    down = jnp.sum(on_diag, axis=1, keepdims=True)
+    across = jnp.sum(on_diag, axis=0, keepdims=True)
+    down = 1.0 / jnp.sqrt(jnp.where(row[:, :1] < count, down, 1.0))
+    across = 1.0 / jnp.sqrt(jnp.where(col[:1] < count, across, 1.0))
+    work = gram * down * across
+    work = jnp.where(col == row + NCOL, 1.0, work)
+    for i in range(count):
+        lead = work[:, i : i + 1]
+        root = 1.0 / jnp.sqrt(work[i : i + 1, i : i + 1])
+        line = work[i : i + 1, :] * root
+        work = jnp.where(row == i, line, jnp.where(row > i, work - (lead * root) * line, work))
+    return work, across
+
+
+def combine(work, across, fields, c_ref, out_ref, columns):
+    last = columns[-1] + 1
+    for i in range(last):
+        lifted = work[:, NCOL + i : NCOL + i + 1] * across[:, i : i + 1]
+        c_ref[i] = jnp.broadcast_to(lifted, (NCOL, NT))
+
+    def slice_out(a, t):
+        here = slab(t)
+        values = [fields[i // NRHS][a, i % NRHS, here, :] for i in range(last)]
+        for j in columns:
+            total = c_ref[0, j : j + 1, :] * values[0]
+            for i in range(1, j + 1):
+                total = total + c_ref[i, j : j + 1, :] * values[i]
+            out_ref[a, j - columns[0], here, :] = total
+
+    return slice_out
 
 
 def krylov_kernel(
@@ -219,6 +250,7 @@
     y1_ref,
     y2_ref,
     y3_ref,
+    q_ref,
     gram_ref,
     diag_ref,
     face_ref,
@@ -234,7 +266,8 @@
     slab_ref,
     edge_ref,
     pack_ref,
-    m_ref,
+    acc_ref,
+    c_ref,
     first_ref,
     second_ref,
     load_sem,
@@ -347,14 +380,59 @@
     for a in range(NV):
         diag_ref[a, a] = diag_ref[a, a] - SHIFT
 
+    def spread(round_index, value, slots, send, recv, count, me, peer):
+        slots[round_index, me] = value
+        copies = []
+        for offset in range(1, count):
+            copies.append(
+                pltpu.make_async_remote_copy(
+                    src_ref=slots.at[round_index, me],
+                    dst_ref=slots.at[round_index, me],
+                    send_sem=send.at[round_index, offset],
+                    recv_sem=recv.at[round_index, offset],
+                    device_id=peer(offset),
+                    device_id_type=MESH,
+                )
+            )
+        for copy in copies:
+            copy.start()
+        return copies
+
+    def collect(round_index, copies, slots, count):
+        for copy in copies:
+            copy.wait()
+        total = slots[round_index, 0]
+        for index in range(1, count):
+            total = total + slots[round_index, index]
+        return total
+
+    def start_first(index, value):
+        return spread(
+            index, value, first_ref, first_send, first_recv, n_first, me_first, first_peer
+        )
+
+    def start_second(index, copies):
+        value = collect(index, copies, first_ref, n_first)
+        return spread(
+            index, value, second_ref, second_send, second_recv, n_second, chip, second_peer
+        )
+
+    acc_ref[...] = jnp.zeros((NCOL, NCOL, 8, NT), jnp.float32)
+    pending = None
     for k in range(POWERS):
         scale = RAISE if k == 0 else 1.0
         target = ys[k + 1]
+        for j in range(k + 1):
+            gram_block(ys[k], ys[j], acc_ref, k, j)
+        last = k == POWERS - 1
+        if last:
+            pending = start_first(0, gram_columns(acc_ref, range(DONE)))
         apply_inner(
             ys[k], target, diag_ref, face_ref, w_ref, stages, ahead_ref, open_ref, scale
         )
+        if last:
+            pending = start_second(0, pending)
         wait_halo(k)
-        last = k == POWERS - 1
         add_halo(
             target,
             face_ref,
@@ -367,33 +445,20 @@
         if not last:
             send_halo(k + 1, range(4))
 
-    def reduce_over(value, slots, send, recv, count, me, peer):
-        slots[me] = value
-        copies = []
-        for offset in range(1, count):
-            copies.append(
-                pltpu.make_async_remote_copy(
-                    src_ref=slots.at[me],
-                    dst_ref=slots.at[me],
-                    send_sem=send.at[offset],
-                    recv_sem=recv.at[offset],
-                    device_id=peer(offset),
-                    device_id_type=MESH,
-                )
-            )
-        for copy in copies:
-            copy.start()
-        for copy in copies:
-            copy.wait()
-        total = slots[0]
-        for index in range(1, count):
-            total = total + slots[index]
-        return total
-
-    gram = local_gram(ys, m_ref)
-    gram = reduce_over(gram, first_ref, first_send, first_recv, n_first, me_first, first_peer)
-    gram = reduce_over(gram, second_ref, second_send, second_recv, n_second, chip, second_peer)
-    gram_ref[...] = gram
+    for j in range(POWERS + 1):
+        gram_block(ys[POWERS], ys[j], acc_ref, POWERS, j)
+    final = start_first(1, gram_columns(acc_ref, range(DONE, NCOL)))
+    early = collect(0, pending, second_ref, n_second)
+    work, across = eliminate(early, DONE)
+    slice_out = combine(work, across, ys, c_ref, q_ref, range(DONE))
+    final = start_second(1, final)
+
+    def fill(t, carry):
+        slice_out(t // LS, t % LS)
+        return carry
+
+    lax.fori_loop(0, NV * LS, fill, 0)
+    gram_ref[...] = early + collect(1, final, second_ref, n_second)
     for k in range(POWERS):
         for j in range(4):
 
@@ -412,10 +477,11 @@
         functools.partial(krylov_kernel, n_stream, n_radial),
         out_shape=(
             *[pltpu.VMEM((NV, NRHS, ROWS + LR, NT), f32)] * (POWERS + 1),
+            pltpu.VMEM((NV, DONE, ROWS, NT), f32),
             jax.ShapeDtypeStruct((NCOL, NT), f32),
         ),
         in_specs=[hbm] * 4,
-        out_specs=tuple([pl.BlockSpec(memory_space=pltpu.VMEM)] * (POWERS + 2)),
+        out_specs=tuple([pl.BlockSpec(memory_space=pltpu.VMEM)] * (POWERS + 3)),
         scratch_shapes=[
             pltpu.VMEM((NV, NV, ROWS, NT), f32),
             pltpu.VMEM((6, ROWS, NT), f32),
@@ -431,110 +497,71 @@
             pltpu.VMEM((POWERS, 2, NV, NRHS, LR, NT), f32),
             pltpu.VMEM((POWERS, 2, NV, NRHS, LS, NT), f32),
             pltpu.VMEM((POWERS, 2, NV, NRHS, LS, NT), f32),
-            pltpu.VMEM((ROWS, ROWS), f32),
-            pltpu.VMEM((n_first, NCOL, NT), f32),
-            pltpu.VMEM((n_second, NCOL, NT), f32),
+            pltpu.VMEM((NCOL, NCOL, 8, NT), f32),
+            pltpu.VMEM((NCOL, NCOL, NT), f32),
+            pltpu.VMEM((2, n_first, NCOL, NT), f32),
+            pltpu.VMEM((2, n_second, NCOL, NT), f32),
             dma((4,)),
             dma((POWERS, 4)),
             dma((POWERS, 4)),
-            dma((n_first,)),
-            dma((n_first,)),
-            dma((n_second,)),
-            dma((n_second,)),
+            dma((2, n_first)),
+            dma((2, n_first)),
+            dma((2, n_second)),
+            dma((2, n_second)),
         ],
-        compiler_params=pltpu.CompilerParams(collective_id=0, has_side_effects=True, vmem_limit_bytes=55_500_000),
+        compiler_params=pltpu.CompilerParams(collective_id=0, has_side_effects=True, vmem_limit_bytes=47_600_000),
     )(right, diag, face, jac)
 
 
-def factor(gram_ref, r_ref, c_ref):
+def basis_kernel(
+    gram_ref, y0_ref, y1_ref, y2_ref, y3_ref, early_ref, q_hbm, r_ref, c_ref, late_ref, sem
+):
+    copies = [
+        pltpu.make_async_copy(early_ref.at[a], q_hbm.at[a, pl.ds(0, DONE)], sem.at[0, a])
+        for a in range(NV)
+    ]
+    for copy in copies:
+        copy.start()
+    work, across = eliminate(gram_ref[...], NCOL)
     row = lax.broadcasted_iota(jnp.int32, (NCOL, NT), 0)
     col = lax.broadcasted_iota(jnp.int32, (NCOL, NT), 1)
-    twice = gram_ref[...]
-    gram = 0.5 * (twice[:, :NCOL] + twice[:, :NCOL].T)
-    gram = jnp.concatenate([gram, jnp.zeros((NCOL, NT - NCOL), jnp.float32)], axis=1)
-    on_diag = jnp.where(row == col, gram, 0.0)
-    down = 1.0 / jnp.sqrt(jnp.sum(on_diag, axis=1, keepdims=True))
-    across = jnp.sum(on_diag, axis=0, keepdims=True)
-    across = 1.0 / jnp.sqrt(jnp.where(col[:1] < NCOL, across, 1.0))
-    work = gram * down * across
-    work = jnp.where(col == row + NCOL, 1.0, work)
-    for i in range(NCOL):
-        lead = work[:, i : i + 1]
-        root = 1.0 / jnp.sqrt(work[i : i + 1, i : i + 1])
-        line = work[i : i + 1, :] * root
-        work = jnp.where(row == i, line, jnp.where(row > i, work - (lead * root) * line, work))
     r_ref[...] = jnp.where(row <= col, work, 0.0)[:, :NCOL]
-    wide = NCOL * HALF
-    col_of = lax.broadcasted_iota(jnp.int32, (NCOL, wide), 1)
-    row_of = lax.broadcasted_iota(jnp.int32, (NCOL, wide), 0)
-    spread = jnp.where(col_of // HALF == row_of, down, 0.0)
-    repeat_row = lax.broadcasted_iota(jnp.int32, (wide, NCOL), 0)
-    repeat_col = lax.broadcasted_iota(jnp.int32, (wide, NCOL), 1)
-    repeat = jnp.where(repeat_row // HALF == repeat_col, 1.0, 0.0).astype(jnp.float32)
-    lifted = jnp.dot(
-        work[:, NCOL : 2 * NCOL], spread, precision=HIGH, preferred_element_type=jnp.float32
-    )
-    lifted = jnp.dot(repeat, lifted, precision=HIGH, preferred_element_type=jnp.float32)
-    full_row = lax.broadcasted_iota(jnp.int32, (wide, wide), 0)
-    full_col = lax.broadcasted_iota(jnp.int32, (wide, wide), 1)
-    lifted = jnp.where(full_row % HALF == full_col % HALF, lifted, 0.0)
-    head = lifted.astype(jnp.bfloat16)
-    tail = (lifted - head.astype(jnp.float32)).astype(jnp.bfloat16)
-    c_ref[...] = jnp.concatenate([head, head, tail], axis=1)
-
-
-def basis_kernel(slabs, gram_ref, y0_ref, y1_ref, y2_ref, y3_ref, q_ref, r_ref, c_ref):
-    @pl.when(pl.program_id(0) == 0)
-    def _():
-        factor(gram_ref, r_ref, c_ref)
-
-    first = pl.program_id(0) * slabs
-
-    def step(a, carry):
-        for half in range(LR // HALF):
-            columns = []
-            for s in range(slabs):
-                rows = pl.ds(pl.multiple_of((first + s) * LR + half * HALF, HALF), HALF)
-                column = []
-                for y_ref in (y0_ref, y1_ref, y2_ref, y3_ref):
-                    column += [y_ref[a, r, rows, :] for r in range(NRHS)]
-                columns.append(jnp.concatenate(column, axis=0))
-            values = jnp.concatenate(columns, axis=1)
-            head = values.astype(jnp.bfloat16)
-            tail = (values - head.astype(jnp.float32)).astype(jnp.bfloat16)
-            stacked = jnp.concatenate([head, tail, head], axis=0)
-            product = jnp.dot(c_ref[...], stacked, preferred_element_type=jnp.float32)
-            for s in range(slabs):
-                rows = slice(s * LR + half * HALF, s * LR + (half + 1) * HALF)
-                for j in range(NCOL):
-                    q_ref[a, j, rows, :] = product[
-                        j * HALF : (j + 1) * HALF, s * NT : (s + 1) * NT
-                    ]
-        return carry
-
-    lax.fori_loop(0, NV, step, 0)
-
-
-def basis(gram, fields):
-    slabs = BASIS_SLABS
-    rows = slabs * LR
+    fields = (y0_ref, y1_ref, y2_ref, y3_ref)
+    slice_out = combine(work, across, fields, c_ref, late_ref, range(DONE, NCOL))
+    for a in range(NV):
+
+        def fill(t, carry, a=a):
+            slice_out(a, t)
+            return carry
+
+        lax.fori_loop(0, LS, fill, 0)
+        copy = pltpu.make_async_copy(
+            late_ref.at[a], q_hbm.at[a, pl.ds(DONE, NCOL - DONE)], sem.at[1, a]
+        )
+        copy.start()
+        copies.append(copy)
+    for copy in copies:
+        copy.wait()
+
+
+def basis(gram, early, fields):
     f32 = jnp.float32
     vmem = pl.BlockSpec(memory_space=pltpu.VMEM)
     return pl.pallas_call(
-        functools.partial(basis_kernel, slabs),
-        grid=(LS // slabs,),
+        basis_kernel,
         out_shape=(
             jax.ShapeDtypeStruct((NV, NCOL, ROWS, NT), f32),
             jax.ShapeDtypeStruct((NCOL, NCOL), f32),
         ),
-        in_specs=[vmem] * (POWERS + 2),
-        out_specs=(
-            pl.BlockSpec((NV, NCOL, rows, NT), lambda s: (0, 0, s, 0)),
-            pl.BlockSpec((NCOL, NCOL), lambda s: (0, 0)),
-        ),
-        scratch_shapes=[pltpu.VMEM((NCOL * HALF, 3 * NCOL * HALF), jnp.bfloat16)],
-        compiler_params=pltpu.CompilerParams(vmem_limit_bytes=30 * 2**20),
-    )(gram, *fields)
+        in_specs=[vmem] * (POWERS + 3),
+        out_specs=(pl.BlockSpec(memory_space=pltpu.HBM), vmem),
+        scratch_shapes=[
+            pltpu.VMEM((NCOL, NCOL, NT), f32),
+            pltpu.VMEM((NV, NCOL - DONE, ROWS, NT), f32),
+            pltpu.SemaphoreType.DMA((2, NV)),
+        ],
+        compiler_params=pltpu.CompilerParams(vmem_limit_bytes=24 * 2**20),
+    )(gram, *fields, early)
 
 
 def body(n_stream, n_radial, right_side, diag_block, face_coef, jacobians):
@@ -542,8 +569,8 @@
     diag = diag_block.reshape(NV, NV, ROWS, NT)
     face = face_coef.reshape(6, ROWS, NT)
     jac = jnp.transpose(jacobians, (1, 0, 2))
-    *fields, gram = krylov(n_stream, n_radial, right, diag, face, jac)
-    q, r_factor = basis(gram, fields)
+    *fields, early, gram = krylov(n_stream, n_radial, right, diag, face, jac)
+    q, r_factor = basis(gram, early, fields)
     return q.reshape(NV, NCOL, LS, LR, NT), r_factor
 
 

time: 54.8 us -> 52.6 us (0.960)
  Pallas kernels: 53.2 us -> 51 us
    pallas_call x1, Pallas kernels: 12.6 us -> 6.65 us  [basis(): pl.pallas_call(basis_kernel, out_shape=(jax.ShapeDtypeStruct((NV, NCOL, R...]
    pallas_call x1, Pallas kernels: 40.6 us -> 44.4 us  [krylov(): pl.pallas_call(functools.partial(krylov_kernel, n_stream, n_radial), out_...]
where the time goes in v4:
time: 52.6 us; the launch traced here: 52.4 us
  Pallas kernels  51 us (97%)
  local copies, waits for them, and re-layouts  0.69 us (1%)
  between operations  0.65 us (1%)
    pallas_call x1, Pallas kernels, krylov(): pl.pallas_call(functools.partial(krylov_kernel, n_stream, n_radial), out_...  44.4 us
    pallas_call x1, Pallas kernels, basis(): pl.pallas_call(basis_kernel, out_shape=(jax.ShapeDtypeStruct((NV, NCOL, R...  6.65 us

profile of v4, /device:TPU:1, one launch (start us, length us, event | category | flops | bytes accessed | tf_op | source)
XLA Modules:
  0.0 52.4 jit_solution(16605250176789382109)
XLA Ops:
  0.6 44.4 %shard_map.59 = (f32[5,4,272,128]{3,2,1,0:T(8,128)S(1)}, f32[5,4,272,128]{3,2,1,0:T(8,128)S(1)}, f32[5,4,272,128]{3,2,1,0:T(8,128)S(1)}, f32[5,4,272,128]{3,2,1,...) custom-call(f32[5,4,256,128]{3,2,1,0:T(8,128)} %bitcast.6, f32[5,5,256,128]{3,2,1,0:T(8,128)} %bitcast.5, ...), custom_call_target="tpu_custom_call" | custom-call | tf_op jit(solution)/shard_map/pallas_call | solution.py:476
  45.0 0.0 copy-start
  45.0 0.7 %copy-done = f32[16,128]{1,0:T(8,128)S(1)} copy-done((f32[16,128]{1,0:T(8,128)S(1)}, f32[16,128]{1,0:T(8,128)}, u32[]{:S(2)}) %copy-start) | copy-done | bytes 8216
  45.7 6.7 %shard_map.60 = (f32[5,16,256,128]{3,2,1,0:T(8,128)}, f32[16,16]{1,0:T(8,128)}) custom-call(f32[16,128]{1,0:T(8,128)S(1)} %copy-done, f32[5,4,272,128]{3,2,1,0:T(8,128)S(1)} %get-tuple-element.11.y0_ref, f32[5,4,272,128]{3,2,1,0:T(8,128)S(1)} %get-tuple-element.12.y1_ref, f32[5,4,272,128]{3,2,1,0:T(8,128)S(1)} %get-tuple-element.13.y2_ref, ...), custom_call_target="tpu_custom_call" | custom-call | tf_op jit(solution)/shard_map/pallas_call | solution.py:550
Async XLA Ops:
  45.0 0.7 %copy-start = (f32[16,128]{1,0:T(8,128)S(1)}, f32[16,128]{1,0:T(8,128)}, u32[]{:S(2)}) copy-start(f32[16,128]{1,0:T(8,128)} %get-tuple-element.10.gram_ref) | copy-start | bytes 24580

commit v5 on v4

--- a/solution.py
+++ b/solution.py
@@ -20,8 +20,12 @@
 KDIM = 256
 OFFSETS = (0, 0, -1, 1, 0, 0)
 UNROLL = 4
-GRAM_ROWS = 32
-GRAM_CHUNKS = ROWS // GRAM_ROWS
+GRAM_ROWS = 16
+GRAM_UNROLL = 8
+GRAM_STEPS = ROWS // (GRAM_ROWS * GRAM_UNROLL)
+FILL_ROWS = 32
+FILL_UNROLL = 2
+FILL_STEPS = ROWS // (FILL_ROWS * FILL_UNROLL)
 DONE = 12
 RAISE = 2.0**24
 MESH = pl.DeviceIdType.MESH
@@ -170,21 +174,21 @@
     pairs = [(p, q) for p in range(NRHS) for q in range(NRHS) if k != j or q <= p]
 
     def step(t, sums):
-        a = t // GRAM_CHUNKS
-        rows = pl.ds(pl.multiple_of((t % GRAM_CHUNKS) * GRAM_ROWS, GRAM_ROWS), GRAM_ROWS)
-        mine = [left[a, p, rows, :] for p in range(NRHS)]
-        other = mine if k == j else [right[a, q, rows, :] for q in range(NRHS)]
-        fresh = []
-        for index, (p, q) in enumerate(pairs):
-            term = mine[p] * other[q]
-            total = sums[index]
-            for piece in range(GRAM_ROWS // 8):
-                total = total + term[piece * 8 : piece * 8 + 8]
-            fresh.append(total)
-        return tuple(fresh)
+        a = t // GRAM_STEPS
+        sums = list(sums)
+        for u in range(GRAM_UNROLL):
+            start = ((t % GRAM_STEPS) * GRAM_UNROLL + u) * GRAM_ROWS
+            rows = pl.ds(pl.multiple_of(start, GRAM_ROWS), GRAM_ROWS)
+            mine = [left[a, p, rows, :] for p in range(NRHS)]
+            other = mine if k == j else [right[a, q, rows, :] for q in range(NRHS)]
+            for index, (p, q) in enumerate(pairs):
+                term = mine[p] * other[q]
+                for piece in range(GRAM_ROWS // 8):
+                    sums[index] = sums[index] + term[piece * 8 : piece * 8 + 8]
+        return tuple(sums)
 
     empty = tuple(jnp.zeros((8, NT), jnp.float32) for _ in pairs)
-    sums = lax.fori_loop(0, NV * GRAM_CHUNKS, step, empty)
+    sums = lax.fori_loop(0, NV * GRAM_STEPS, step, empty)
     for index, (p, q) in enumerate(pairs):
         acc_ref[4 * k + p, 4 * j + q] = sums[index]
         if k == j and p != q:
@@ -228,7 +232,11 @@
         c_ref[i] = jnp.broadcast_to(lifted, (NCOL, NT))
 
     def slice_out(a, t):
-        here = slab(t)
+        for u in range(FILL_UNROLL):
+            part_out(a, (t * FILL_UNROLL + u) * FILL_ROWS)
+
+    def part_out(a, start):
+        here = pl.ds(pl.multiple_of(start, FILL_ROWS), FILL_ROWS)
         values = [fields[i // NRHS][a, i % NRHS, here, :] for i in range(last)]
         for j in columns:
             total = c_ref[0, j : j + 1, :] * values[0]
@@ -375,6 +383,8 @@
             for r in range(NRHS):
                 pack_ref[0, side, a, r] = y0_ref[a, r, rows, :]
     send_halo(0, (2, 3))
+    acc_ref[...] = jnp.zeros((NCOL, NCOL, 8, NT), jnp.float32)
+    gram_block(y0_ref, y0_ref, acc_ref, 0, 0)
     loads[1].wait()
     loads[2].wait()
     for a in range(NV):
@@ -417,12 +427,11 @@
             index, value, second_ref, second_send, second_recv, n_second, chip, second_peer
         )
 
-    acc_ref[...] = jnp.zeros((NCOL, NCOL, 8, NT), jnp.float32)
     pending = None
     for k in range(POWERS):
         scale = RAISE if k == 0 else 1.0
         target = ys[k + 1]
-        for j in range(k + 1):
+        for j in range(k + 1 if k else 0):
             gram_block(ys[k], ys[j], acc_ref, k, j)
         last = k == POWERS - 1
         if last:
@@ -454,10 +463,10 @@
     final = start_second(1, final)
 
     def fill(t, carry):
-        slice_out(t // LS, t % LS)
+        slice_out(t // FILL_STEPS, t % FILL_STEPS)
         return carry
 
-    lax.fori_loop(0, NV * LS, fill, 0)
+    lax.fori_loop(0, NV * FILL_STEPS, fill, 0)
     gram_ref[...] = early + collect(1, final, second_ref, n_second)
     for k in range(POWERS):
         for j in range(4):
@@ -478,7 +487,7 @@
         out_shape=(
             *[pltpu.VMEM((NV, NRHS, ROWS + LR, NT), f32)] * (POWERS + 1),
             pltpu.VMEM((NV, DONE, ROWS, NT), f32),
-            jax.ShapeDtypeStruct((NCOL, NT), f32),
+            pltpu.VMEM((NCOL, NT), f32),
         ),
         in_specs=[hbm] * 4,
         out_specs=tuple([pl.BlockSpec(memory_space=pltpu.VMEM)] * (POWERS + 3)),
@@ -534,7 +543,7 @@
             slice_out(a, t)
             return carry
 
-        lax.fori_loop(0, LS, fill, 0)
+        lax.fori_loop(0, FILL_STEPS, fill, 0)
         copy = pltpu.make_async_copy(
             late_ref.at[a], q_hbm.at[a, pl.ds(DONE, NCOL - DONE)], sem.at[1, a]
         )

time: 52.6 us -> 46.8 us (0.89)
  Pallas kernels: 51 us -> 46.1 us
  local copies, waits for them, and re-layouts: 0.69 us -> 0 us
    pallas_call x1, Pallas kernels: 44.4 us -> 39.8 us  [krylov(): pl.pallas_call(functools.partial(krylov_kernel, n_stream, n_radial), out_...]
    unnamed x2 -> x0, local copies, waits for them, and re-layouts: 0.69 us -> none
where the time goes in v5:
time: 46.8 us; the launch traced here: 46.7 us
  Pallas kernels  46.1 us (99%)
  between operations  0.64 us (1%)
    pallas_call x1, Pallas kernels, krylov(): pl.pallas_call(functools.partial(krylov_kernel, n_stream, n_radial), out_...  39.8 us
    pallas_call x1, Pallas kernels, basis(): pl.pallas_call(basis_kernel, out_shape=(jax.ShapeDtypeStruct((NV, NCOL, R...  6.27 us

profile of v5, /device:TPU:1, one launch (start us, length us, event | category | flops | bytes accessed | tf_op | source)
XLA Modules:
  0.0 46.7 jit_solution(1088066586481437244)
XLA Ops:
  0.6 39.8 %shard_map.59 = (f32[5,4,272,128]{3,2,1,0:T(8,128)S(1)}, f32[5,4,272,128]{3,2,1,0:T(8,128)S(1)}, f32[5,4,272,128]{3,2,1,0:T(8,128)S(1)}, f32[5,4,272,128]{3,2,1,...) custom-call(f32[5,4,256,128]{3,2,1,0:T(8,128)} %bitcast.6, f32[5,5,256,128]{3,2,1,0:T(8,128)} %bitcast.5, ...), custom_call_target="tpu_custom_call" | custom-call | tf_op jit(solution)/shard_map/pallas_call | solution.py:485
  40.4 6.3 %shard_map.60 = (f32[5,16,256,128]{3,2,1,0:T(8,128)}, f32[16,16]{1,0:T(8,128)}) custom-call(f32[16,128]{1,0:T(8,128)S(1)} %get-tuple-element.10.gram_ref, f32[5,4,272,128]{3,2,1,0:T(8,128)S(1)} %get-tuple-element.11.y0_ref, f32[5,4,272,128]{3,2,1,0:T(8,128)S(1)} %get-tuple-element.12.y1_ref, f32[5,4,272,128]{3,2,1,0:T(8,128)S(1)} %get-tuple-element.13.y2_ref, ...), custom_call_target="tpu_custom_call" | custom-call | tf_op jit(solution)/shard_map/pallas_call | solution.py:559

commit v6 on v5

--- a/solution.py
+++ b/solution.py
@@ -20,6 +20,7 @@
 KDIM = 256
 OFFSETS = (0, 0, -1, 1, 0, 0)
 UNROLL = 4
+DIAG_ROWS = UNROLL * LR
 GRAM_ROWS = 16
 GRAM_UNROLL = 8
 GRAM_STEPS = ROWS // (GRAM_ROWS * GRAM_UNROLL)
@@ -93,13 +94,17 @@
                 stage[a, r, half * 8 : half * 8 + 8, :] = totals[r]
 
 
-def apply_inner(source, target, diag_ref, face_ref, w_ref, stages, ahead_ref, open_ref, scale):
+def apply_inner(
+    source, target, diag_ref, face_ref, w_ref, stages, ahead_ref, open_ref, scale, prepare=None
+):
     cells = [(a, r) for a in range(NV) for r in range(NRHS)]
     ahead_ref[...] = jnp.zeros((NV, NRHS, LR, NT), jnp.float32)
     open_ref[...] = jnp.zeros((NV, NRHS, LR, NT), jnp.float32)
 
     def step(t, carry):
         s0 = t * UNROLL
+        if prepare is not None:
+            prepare(t)
         for u in range(UNROLL):
             apply_blocks(source, diag_ref, stages[u], s0 + u, scale)
         ahead = {cell: ahead_ref[cell[0], cell[1]] for cell in cells}
@@ -218,10 +223,10 @@
     work = gram * down * across
     work = jnp.where(col == row + NCOL, 1.0, work)
     for i in range(count):
-        lead = work[:, i : i + 1]
-        root = 1.0 / jnp.sqrt(work[i : i + 1, i : i + 1])
-        line = work[i : i + 1, :] * root
-        work = jnp.where(row == i, line, jnp.where(row > i, work - (lead * root) * line, work))
+        line = work[i : i + 1, :] * (1.0 / work[i : i + 1, i : i + 1])
+        work = jnp.where(row > i, work - work[:, i : i + 1] * line, work)
+    pivots = jnp.sum(jnp.where(row == col, work, 0.0), axis=1, keepdims=True)
+    work = work * (1.0 / jnp.sqrt(jnp.where(row[:, :1] < count, pivots, 1.0)))
     return work, across
 
 
@@ -306,27 +311,42 @@
     loads = [
         pltpu.make_async_copy(right_hbm, y0_ref.at[:, :, pl.ds(0, ROWS), :], load_sem.at[0]),
         pltpu.make_async_copy(face_hbm, face_ref, load_sem.at[1]),
-        pltpu.make_async_copy(diag_hbm, diag_ref, load_sem.at[2]),
-        pltpu.make_async_copy(jac_hbm, jac_ref, load_sem.at[3]),
+        pltpu.make_async_copy(jac_hbm, jac_ref, load_sem.at[2]),
     ]
-    for load in loads:
-        load.start()
+
+    def diag_load(t):
+        rows = pl.ds(pl.multiple_of(t * DIAG_ROWS, DIAG_ROWS), DIAG_ROWS)
+        return pltpu.make_async_copy(
+            diag_hbm.at[:, :, rows, :], diag_ref.at[:, :, rows, :], load_sem.at[3 + t]
+        )
+
+    def diag_ready(t):
+        rows = pl.ds(pl.multiple_of(t * DIAG_ROWS, DIAG_ROWS), DIAG_ROWS)
+        diag_load(t).wait()
+        for a in range(NV):
+            diag_ref[a, a, rows, :] = diag_ref[a, a, rows, :] - SHIFT
+
+    loads[2].start()
+    loads[0].start()
+    loads[1].start()
+    for t in range(LS // UNROLL):
+        diag_load(t).start()
 
     barrier = pltpu.get_barrier_semaphore()
+    peers = ((si + 1, ri), (si - 1, ri), (si, ri + 1), (si, ri - 1))
+    present = (si < n_stream - 1, si > 0, ri < n_radial - 1, ri > 0)
+    source_of = (1, 0, 3, 2)
+    for j in range(4):
+
+        @pl.when(present[j])
+        def _(j=j):
+            pl.semaphore_signal(barrier, inc=1, device_id=peers[j], device_id_type=MESH)
+
     for offset in range(1, n_first):
         pl.semaphore_signal(barrier, inc=1, device_id=first_peer(offset), device_id_type=MESH)
     for offset in range(1, n_second):
         pl.semaphore_signal(barrier, inc=1, device_id=second_peer(offset), device_id_type=MESH)
-    peers = ((si + 1, ri), (si - 1, ri), (si, ri + 1), (si, ri - 1))
-    present = (si < n_stream - 1, si > 0, ri < n_radial - 1, ri > 0)
-    source_of = (1, 0, 3, 2)
-    for j in range(4):
-
-        @pl.when(present[j])
-        def _(j=j):
-            pl.semaphore_signal(barrier, inc=1, device_id=peers[j], device_id_type=MESH)
-
-    loads[3].wait()
+    loads[2].wait()
     build_operator(jac_ref, w_ref, halo_w_ref)
     for side in range(2):
 
@@ -386,10 +406,6 @@
     acc_ref[...] = jnp.zeros((NCOL, NCOL, 8, NT), jnp.float32)
     gram_block(y0_ref, y0_ref, acc_ref, 0, 0)
     loads[1].wait()
-    loads[2].wait()
-    for a in range(NV):
-        diag_ref[a, a] = diag_ref[a, a] - SHIFT
-
     def spread(round_index, value, slots, send, recv, count, me, peer):
         slots[round_index, me] = value
         copies = []
@@ -437,7 +453,16 @@
         if last:
             pending = start_first(0, gram_columns(acc_ref, range(DONE)))
         apply_inner(
-            ys[k], target, diag_ref, face_ref, w_ref, stages, ahead_ref, open_ref, scale
+            ys[k],
+            target,
+            diag_ref,
+            face_ref,
+            w_ref,
+            stages,
+            ahead_ref,
+            open_ref,
+            scale,
+            diag_ready if k == 0 else None,
         )
         if last:
             pending = start_second(0, pending)
@@ -452,7 +477,7 @@
             scale,
         )
         if not last:
-            send_halo(k + 1, range(4))
+            send_halo(k + 1, (2, 3, 0, 1))
 
     for j in range(POWERS + 1):
         gram_block(ys[POWERS], ys[j], acc_ref, POWERS, j)
@@ -460,13 +485,14 @@
     early = collect(0, pending, second_ref, n_second)
     work, across = eliminate(early, DONE)
     slice_out = combine(work, across, ys, c_ref, q_ref, range(DONE))
-    final = start_second(1, final)
 
     def fill(t, carry):
         slice_out(t // FILL_STEPS, t % FILL_STEPS)
         return carry
 
-    lax.fori_loop(0, NV * FILL_STEPS, fill, 0)
+    lax.fori_loop(0, FILL_STEPS, fill, 0)
+    final = start_second(1, final)
+    lax.fori_loop(FILL_STEPS, NV * FILL_STEPS, fill, 0)
     gram_ref[...] = early + collect(1, final, second_ref, n_second)
     for k in range(POWERS):
         for j in range(4):
@@ -510,7 +536,7 @@
             pltpu.VMEM((NCOL, NCOL, NT), f32),
             pltpu.VMEM((2, n_first, NCOL, NT), f32),
             pltpu.VMEM((2, n_second, NCOL, NT), f32),
-            dma((4,)),
+            dma((3 + LS // UNROLL,)),
             dma((POWERS, 4)),
             dma((POWERS, 4)),
             dma((2, n_first)),

time: 46.8 us -> 47 us (level)
  no operation moved by 1% of the time
where the time goes in v6:
time: 47 us; the launch traced here: 46.5 us
  Pallas kernels  45.9 us (98%)
  between operations  0.64 us (1%)
    pallas_call x1, Pallas kernels, krylov(): pl.pallas_call(functools.partial(krylov_kernel, n_stream, n_radial), out_...  39.8 us
    pallas_call x1, Pallas kernels, basis(): pl.pallas_call(basis_kernel, out_shape=(jax.ShapeDtypeStruct((NV, NCOL, R...  6.11 us

profile of v6, /device:TPU:1, one launch (start us, length us, event | category | flops | bytes accessed | tf_op | source)
XLA Modules:
  0.0 46.5 jit_solution(753369824257591562)
XLA Ops:
  0.6 39.8 %shard_map.59 = (f32[5,4,272,128]{3,2,1,0:T(8,128)S(1)}, f32[5,4,272,128]{3,2,1,0:T(8,128)S(1)}, f32[5,4,272,128]{3,2,1,0:T(8,128)S(1)}, f32[5,4,272,128]{3,2,1,...) custom-call(f32[5,4,256,128]{3,2,1,0:T(8,128)} %bitcast.6, f32[5,5,256,128]{3,2,1,0:T(8,128)} %bitcast.5, ...), custom_call_target="tpu_custom_call" | custom-call | tf_op jit(solution)/shard_map/pallas_call | solution.py:511
  40.4 6.1 %shard_map.60 = (f32[5,16,256,128]{3,2,1,0:T(8,128)}, f32[16,16]{1,0:T(8,128)}) custom-call(f32[16,128]{1,0:T(8,128)S(1)} %get-tuple-element.10.gram_ref, f32[5,4,272,128]{3,2,1,0:T(8,128)S(1)} %get-tuple-element.11.y0_ref, f32[5,4,272,128]{3,2,1,0:T(8,128)S(1)} %get-tuple-element.12.y1_ref, f32[5,4,272,128]{3,2,1,0:T(8,128)S(1)} %get-tuple-element.13.y2_ref, ...), custom_call_target="tpu_custom_call" | custom-call | tf_op jit(solution)/shard_map/pallas_call | solution.py:585

commit v7 on v6

--- a/solution.py
+++ b/solution.py
@@ -143,12 +143,13 @@
     target[:, :, ROWS - LR : ROWS, :] = open_ref[...]
 
 
-def add_halo(target, face_ref, halo_w_ref, slabs, edges, rows_ref, scale):
+def add_halo(target, face_ref, halo_w_ref, slabs, edges, rows_ref, scale, arrive, leave):
+    arrive((0, 1))
     for side in range(2):
         start = 0 if side == 0 else ROWS - LR
         product = jnp.dot(
             halo_w_ref[side * BLK : (side + 1) * BLK, :],
-            split_fields(slabs[side]),
+            split_fields(slabs[side][...]),
             preferred_element_type=jnp.float32,
         )
         weight = face_ref[side, start : start + LR, :] * scale
@@ -158,10 +159,11 @@
                     weight * product[a * LR : (a + 1) * LR, r * NT : (r + 1) * NT]
                 )
     for side in range(2):
+        arrive((2 + side,))
         rows = pl.ds(0 if side == 0 else LR - 1, LS, stride=LR)
         product = jnp.dot(
             halo_w_ref[(2 + side) * BLK : (3 + side) * BLK, :],
-            split_fields(edges[side]),
+            split_fields(edges[side][...]),
             preferred_element_type=jnp.float32,
         )
         weight = face_ref[2 + side, rows, :] * scale
@@ -173,6 +175,8 @@
                 target[a, r, rows, :] = fresh
                 if rows_ref is not None:
                     rows_ref[side, a, r] = fresh
+        leave((3 - side,))
+    leave((0, 1))
 
 
 def gram_block(left, right, acc_ref, k, j):
@@ -388,8 +392,8 @@
             def _(j=j):
                 halo_copy(k, j).start()
 
-    def wait_halo(k):
-        for j in range(4):
+    def wait_halo(k, js):
+        for j in js:
 
             @pl.when(present[source_of[j]])
             def _(j=j):
@@ -466,18 +470,17 @@
         )
         if last:
             pending = start_second(0, pending)
-        wait_halo(k)
         add_halo(
             target,
             face_ref,
             halo_w_ref,
-            (slab_ref[k, 0], slab_ref[k, 1]),
-            (edge_ref[k, 0], edge_ref[k, 1]),
+            (slab_ref.at[k, 0], slab_ref.at[k, 1]),
+            (edge_ref.at[k, 0], edge_ref.at[k, 1]),
             None if last else pack_ref.at[k + 1],
             scale,
-        )
-        if not last:
-            send_halo(k + 1, (2, 3, 0, 1))
+            functools.partial(wait_halo, k),
+            (lambda js: None) if last else functools.partial(send_halo, k + 1),
+        )
 
     for j in range(POWERS + 1):
         gram_block(ys[POWERS], ys[j], acc_ref, POWERS, j)

time: 47 us -> 46.7 us (level)
  no operation moved by 1% of the time
where the time goes in v7:
time: 46.7 us; the launch traced here: 46.5 us
  Pallas kernels  45.9 us (98%)
  between operations  0.64 us (1%)
    pallas_call x1, Pallas kernels, krylov(): pl.pallas_call(functools.partial(krylov_kernel, n_stream, n_radial), out_...  39.7 us
    pallas_call x1, Pallas kernels, basis(): pl.pallas_call(basis_kernel, out_shape=(jax.ShapeDtypeStruct((NV, NCOL, R...  6.11 us

profile of v7, /device:TPU:1, one launch (start us, length us, event | category | flops | bytes accessed | tf_op | source)
XLA Modules:
  0.0 46.5 jit_solution(2819578676100439851)
XLA Ops:
  0.6 39.7 %shard_map.59 = (f32[5,4,272,128]{3,2,1,0:T(8,128)S(1)}, f32[5,4,272,128]{3,2,1,0:T(8,128)S(1)}, f32[5,4,272,128]{3,2,1,0:T(8,128)S(1)}, f32[5,4,272,128]{3,2,1,...) custom-call(f32[5,4,256,128]{3,2,1,0:T(8,128)} %bitcast.6, f32[5,5,256,128]{3,2,1,0:T(8,128)} %bitcast.5, ...), custom_call_target="tpu_custom_call" | custom-call | tf_op jit(solution)/shard_map/pallas_call | solution.py:514
  40.4 6.1 %shard_map.60 = (f32[5,16,256,128]{3,2,1,0:T(8,128)}, f32[16,16]{1,0:T(8,128)}) custom-call(f32[16,128]{1,0:T(8,128)S(1)} %get-tuple-element.10.gram_ref, f32[5,4,272,128]{3,2,1,0:T(8,128)S(1)} %get-tuple-element.11.y0_ref, f32[5,4,272,128]{3,2,1,0:T(8,128)S(1)} %get-tuple-element.12.y1_ref, f32[5,4,272,128]{3,2,1,0:T(8,128)S(1)} %get-tuple-element.13.y2_ref, ...), custom_call_target="tpu_custom_call" | custom-call | tf_op jit(solution)/shard_map/pallas_call | solution.py:588
